TPU v7x, 256 devices: a whole 4x4x8 slice. The times are simulated.
256 devices in a mesh: dp: 8 (over y, core), seq: 32 (over x, z).
Axes of the slice: x: 4, y: 4, z: 8, core: 2. Of those that a mesh axis runs over, the one named last changes fastest.
Arguments:
- token_ids: int32 [8, 4096], P('dp', 'seq'), may hold values from 0 to 255
- cotangent: bfloat16 [8, 4096, 768], P('dp', 'seq'), may hold values from -6 to 6
- table: bfloat16 [256, 768], replicated, may hold values from -12 to 12
- w_query: bfloat16 [768, 768], replicated, may hold values from -2 to 2
- w_key: bfloat16 [768, 768], replicated, may hold values from -2 to 2
- w_value: bfloat16 [768, 768], replicated, may hold values from -0.21875 to 0.21875
- w_out: bfloat16 [768, 768], replicated, may hold values from -0.21875 to 0.21875
- window: int32 [12], replicated, may hold values from 64 to 512, as said below
Outputs:
- grad_input: bfloat16 [8, 4096, 768], P('dp', 'seq')
- weight_grads: float32 [3072, 768], P('seq')
Inputs may be any that keep to these rules, and one draw needn't show every extreme that they name: Some head's window is exactly 512.
All inputs are finite; a program needn't handle non-finite values.
Results may differ from a plain program's by a relative error of at most 0.025.
Values may be sent and summed in bfloat16 or wider, within the bound.
A program may use at most 128 MiB of HBM per device.

v0:
```python
import jax
import jax.numpy as jnp
from jax import lax
from jax.sharding import PartitionSpec as P

HEADS = 12
HEAD_DIM = 64
WINDOW = 512


EPSILON = 1e-05


def shifted(block, axis, distance):
    devices = range(lax.axis_size(axis))
    route = [(i - distance, i) for i in devices if i - distance in devices]
    return lax.ppermute(block, axis, route)


def rotate(values, positions):
    row_count = values.shape[0]
    shaped = values.reshape(row_count, -1, HEAD_DIM)
    middle = HEAD_DIM // 2
    frequency = 10000.0 ** (-2.0 * jnp.arange(middle, dtype=jnp.float32) / HEAD_DIM)
    angles = positions.astype(jnp.float32)[:, None] * frequency[None, :]
    cosine = jnp.cos(angles)[:, None, :]
    sine_part = jnp.sin(angles)[:, None, :]
    former = shaped[..., :middle]
    latter = shaped[..., middle:]
    turned = jnp.concatenate(
        [former * cosine - latter * sine_part, latter * cosine + former * sine_part], axis=-1
    )
    return turned.reshape(row_count, -1)


def unrotate(values, positions):
    row_count = values.shape[0]
    shaped = values.reshape(row_count, -1, HEAD_DIM)
    middle = HEAD_DIM // 2
    frequency = 10000.0 ** (-2.0 * jnp.arange(middle, dtype=jnp.float32) / HEAD_DIM)
    angles = positions.astype(jnp.float32)[:, None] * frequency[None, :]
    cosine = jnp.cos(angles)[:, None, :]
    sine_part = jnp.sin(angles)[:, None, :]
    former = shaped[..., :middle]
    latter = shaped[..., middle:]
    turned = jnp.concatenate(
        [former * cosine + latter * sine_part, latter * cosine - former * sine_part], axis=-1
    )
    return turned.reshape(row_count, -1)


def tdot(left, right):
    return lax.dot_general(
        left, right, (((0,), (0,)), ((), ())), preferred_element_type=jnp.float32
    )


def ndot(left, right):
    return lax.dot_general(
        left, right, (((1,), (1,)), ((), ())), preferred_element_type=jnp.float32
    )


def embed_rows(byte_ids, table):
    onehot = (byte_ids[:, None] == jnp.arange(table.shape[0], dtype=jnp.int32)[None, :]).astype(
        jnp.bfloat16
    )
    return jnp.dot(onehot, table, preferred_element_type=jnp.float32).astype(jnp.bfloat16)


def normalize(embedded):
    widened = embedded.astype(jnp.float32)
    inv_rms = lax.rsqrt(jnp.mean(widened * widened, axis=1, keepdims=True) + EPSILON)
    return (widened, inv_rms, (widened * inv_rms).astype(jnp.bfloat16))


def keys_values(normed, positions, w_key, w_value):
    key_rows = rotate(jnp.dot(normed, w_key, preferred_element_type=jnp.float32), positions).astype(
        jnp.bfloat16
    )
    value_rows = jnp.dot(normed, w_value, preferred_element_type=jnp.float32).astype(jnp.bfloat16)
    return (key_rows, value_rows)


def head_group(
    query_heads, key_heads, value_heads, grad_heads, group_window, own_pos, key_pos, score_scale
):
    distance = own_pos[:, None] - key_pos[None, :]
    allowed = (
        (distance[None] >= 0)
        & (distance[None] < group_window[:, None, None])
        & (key_pos[None, None, :] >= 0)
    )
    scores = (
        jnp.einsum("qhd,khd->hqk", query_heads, key_heads, preferred_element_type=jnp.float32)
        * score_scale
    )
    masked = jnp.where(allowed, scores, -1e30)
    row_max = jnp.max(masked, axis=-1, keepdims=True)
    weights = jnp.where(allowed, jnp.exp(masked - row_max), 0.0)
    probs = weights / jnp.sum(weights, axis=-1, keepdims=True)
    probs_b = probs.astype(jnp.bfloat16)
    attended = jnp.einsum(
        "hqk,khd->qhd", probs_b, value_heads, preferred_element_type=jnp.float32
    ).astype(jnp.bfloat16)
    grad_probs = jnp.einsum(
        "qhd,khd->hqk", grad_heads, value_heads, preferred_element_type=jnp.float32
    )
    row_term = jnp.sum(probs * grad_probs, axis=-1, keepdims=True)
    grad_scores = (probs * (grad_probs - row_term) * score_scale).astype(jnp.bfloat16)
    grad_query = jnp.einsum(
        "hqk,khd->qhd", grad_scores, key_heads, preferred_element_type=jnp.float32
    )
    grad_key = jnp.einsum(
        "hqk,qhd->khd", grad_scores, query_heads, preferred_element_type=jnp.float32
    )
    grad_value = jnp.einsum("hqk,qhd->khd", probs_b, grad_heads, preferred_element_type=jnp.float32)
    return (attended, grad_query, grad_key, grad_value)


def on_device(token_ids, cotangent, table, w_query, w_key, w_value, w_out, window):
    local_ids = token_ids[0]
    grad_out = cotangent[0]
    length = local_ids.shape[0]
    features = table.shape[1]
    tail_rows = min(length, WINDOW)
    reach_devs = -(-WINDOW // length)
    halo_rows = reach_devs * tail_rows
    offset = lax.axis_index("seq") * length
    own_pos = offset + jnp.arange(length, dtype=jnp.int32)
    halo_pos = offset - halo_rows + jnp.arange(halo_rows, dtype=jnp.int32)
    score_scale = HEAD_DIM ** (-0.5)
    embedded = embed_rows(local_ids, table)
    widened, inv_rms, normed = normalize(embedded)
    query = rotate(jnp.dot(normed, w_query, preferred_element_type=jnp.float32), own_pos).astype(
        jnp.bfloat16
    )
    key_own, value_own = keys_values(normed, own_pos, w_key, w_value)
    key_pieces = []
    value_pieces = []
    for hop_index in range(reach_devs):
        far_keys, far_values = shifted((key_own, value_own), "seq", hop_index + 1)
        key_pieces.insert(0, far_keys)
        value_pieces.insert(0, far_values)
    key_halo = jnp.concatenate(key_pieces, axis=0)
    value_halo = jnp.concatenate(value_pieces, axis=0)
    span_rows = halo_rows + length
    key_all = jnp.concatenate([key_halo, key_own], axis=0)
    value_all = jnp.concatenate([value_halo, value_own], axis=0)
    key_pos = jnp.concatenate([halo_pos, own_pos], axis=0)
    query_heads = query.reshape(length, HEADS, HEAD_DIM)
    key_heads = key_all.reshape(span_rows, HEADS, HEAD_DIM)
    value_heads = value_all.reshape(span_rows, HEADS, HEAD_DIM)
    grad_att = ndot(grad_out, w_out).astype(jnp.bfloat16)
    grad_heads = grad_att.reshape(length, HEADS, HEAD_DIM)
    group_size = 4
    attended_parts = []
    query_parts = []
    key_parts = []
    value_parts = []
    for group_index in range(HEADS // group_size):
        lower = group_index * group_size
        upper = lower + group_size
        outputs = head_group(
            query_heads[:, lower:upper],
            key_heads[:, lower:upper],
            value_heads[:, lower:upper],
            grad_heads[:, lower:upper],
            window[lower:upper],
            own_pos,
            key_pos,
            score_scale,
        )
        attended_parts.append(outputs[0])
        query_parts.append(outputs[1])
        key_parts.append(outputs[2])
        value_parts.append(outputs[3])
    attended = jnp.concatenate(attended_parts, axis=1).reshape(length, features)
    grad_query = jnp.concatenate(query_parts, axis=1).reshape(length, features)
    grad_key = jnp.concatenate(key_parts, axis=1).reshape(span_rows, features)
    grad_value = jnp.concatenate(value_parts, axis=1).reshape(span_rows, features)
    tail_keys = grad_key[:halo_rows].reshape(reach_devs, tail_rows, features)
    tail_values = grad_value[:halo_rows].reshape(reach_devs, tail_rows, features)
    back_keys = jnp.zeros((tail_rows, features), jnp.float32)
    back_values = jnp.zeros((tail_rows, features), jnp.float32)
    for hop_index in range(reach_devs):
        got_keys, got_values = shifted(
            (tail_keys[reach_devs - 1 - hop_index], tail_values[reach_devs - 1 - hop_index]),
            "seq",
            -(hop_index + 1),
        )
        back_keys = back_keys + got_keys
        back_values = back_values + got_values
    own_keys = grad_key[halo_rows:]
    own_values = grad_value[halo_rows:]
    own_keys = jnp.concatenate([own_keys[: length - tail_rows], own_keys + back_keys], axis=0)
    own_values = jnp.concatenate(
        [own_values[: length - tail_rows], own_values + back_values], axis=0
    )
    grad_q_lin = unrotate(grad_query, own_pos).astype(jnp.bfloat16)
    grad_k_lin = unrotate(own_keys, own_pos).astype(jnp.bfloat16)
    grad_v_lin = own_values.astype(jnp.bfloat16)
    grad_normed = ndot(grad_q_lin, w_query) + ndot(grad_k_lin, w_key) + ndot(grad_v_lin, w_value)
    scaled = widened * inv_rms
    grad_input = (
        inv_rms * (grad_normed - scaled * jnp.mean(grad_normed * scaled, axis=1, keepdims=True))
    ).astype(jnp.bfloat16)
    term = jnp.concatenate(
        [
            tdot(normed, grad_q_lin),
            tdot(normed, grad_k_lin),
            tdot(normed, grad_v_lin),
            tdot(attended, grad_out),
        ],
        axis=0,
    )
    shares = lax.psum_scatter(term.astype(jnp.bfloat16), "seq", scatter_dimension=0, tiled=True)
    weight_grads = lax.psum(shares, "dp").astype(jnp.float32)
    return (grad_input[None], weight_grads)


def solution(mesh):
    return jax.shard_map(
        on_device,
        mesh=mesh,
        in_specs=(P("dp", "seq"), P("dp", "seq", None), P(), P(), P(), P(), P(), P()),
        out_specs=(P("dp", "seq", None), P("seq", None)),
        check_vma=False,
    )
```

profile of v0, /device:TPU:1, one launch (start us, length us, event | category | flops | bytes accessed | tf_op | source)
XLA Modules:
  0.0 591.0 jit_solution(5560135934124274321)
XLA Ops:
  7.2 1.5 multiply_reduce_fusion.4
  10.5 5.0 collective-permute-start.7
  15.5 4.9 collective-permute-start.6
  20.4 5.7 collective-permute-start.5
  26.1 3.1 collective-permute-start.4
  32.8 4.2 collective-permute-start.3
  38.4 2.5 convolution_convert_fusion.5
  40.9 1.4 fusion.102
  44.7 10.0 %collective-permute-start.2 = (bf16[128,768]{0,1:T(8,128)(2,1)}, bf16[128,768]{0,1:T(8,128)(2,1)}, u32[]{:S(2)}, u32[]{:S(2)}) collective-permute-start(bf16[128,768]{0,1:T(8,128)(2,1)} %bitcast.2), channel_id=1, source_target_pairs={{0,2},{1,3},{2,4},{3,5},{4,6},{5,7},{6,8},{7,9},{8,10},{9,11},{10,... | collective-permute-start | bytes 589832 | tf_op jit(solution)/shard_map/ppermute | solution.py:17
  54.7 1.6 constant_dynamic-update-slice_fusion.9
  56.3 2.0 collective-permute-start.1
  58.3 1.6 constant_dynamic-update-slice_fusion.8
  59.9 7.9 %collective-permute-start = (bf16[128,768]{0,1:T(8,128)(2,1)}, bf16[128,768]{0,1:T(8,128)(2,1)}, u32[]{:S(2)}, u32[]{:S(2)}) collective-permute-start(bf16[128,768]{0,1:T(8,128)(2,1)} %bitcast.2), channel_id=1, source_target_pairs={{0,4},{1,5},{2,6},{3,7},{4,8},{5,9},{6,10},{7,11},{8,12},{9,13},{1... | collective-permute-start | bytes 589832 | tf_op jit(solution)/shard_map/ppermute | solution.py:17
  67.9 1.6 constant_dynamic-update-slice_fusion.7
  69.5 1.6 constant_dynamic-update-slice_fusion.6
  71.1 1.6 constant_dynamic-update-slice_fusion.5
  72.7 2.3 copy.23
  75.0 4.5 collective-permute-done
  80.4 2.4 fusion.68
  83.8 1.5 fusion.71
  86.3 1.5 fusion.74
  94.1 6.0 %fusion.55 = f32[128,4,64]{0,2,1:T(8,128)} fusion(bf16[640,12,64]{0,2,1:T(8,128)(2,1)} %bitcast.121, f32[4,128,640]{2,1,0:T(8,128)} %fusion.68, f32[4,128,640]{2,1,0:T(8,128)} %copy-done.8, f32[4,128]{1,0:T(4,128)} %copy-done.43), kind=kOutput, calls=%fused_computation.66 | convolution fusion | flops 44237952 | bytes 3737600 | tf_op jit(solution)/shard_map/hqk,khd->qhd/dot_general | solution.py:111
  100.1 6.1 %convolution_bitcast_fusion.3 = f32[640,4,64]{0,2,1:T(8,128)} fusion(f32[4,128,640]{2,1,0:T(8,128)} %fusion.68, bf16[128,12,32]{0,2,1:T(8,128)(2,1)} %get-tuple-element.17, bf16[128,12,32]{0,2,1:T(8,128)(2,1)} %get-tuple-element.16, f32[4,128,640]{2,1,0:T(8,128)} %copy-done.8, f32[4,128]{1,0:T(4,128)} %copy-done.43), kind=kOutput, calls=%fused_computation.46 | convolution fusion | flops 44631168 | bytes 3475456 | tf_op jit(solution)/shard_map/hqk,qhd->khd/dot_general | solution.py:114
  106.2 2.6 convolution_bitcast_fusion
  108.8 1.5 fusion.16
  113.2 5.8 fusion.52
  119.0 6.0 %convolution_bitcast_fusion.4 = f32[640,4,64]{0,2,1:T(8,128)} fusion(f32[4,128,640]{2,1,0:T(8,128)} %fusion.71, bf16[128,12,32]{0,2,1:T(8,128)(2,1)} %get-tuple-element.17, bf16[128,12,32]{0,2,1:T(8,128)(2,1)} %get-tuple-element.16, f32[4,128,640]{2,1,0:T(8,128)} %copy-done.9, f32[4,128]{1,0:T(4,128)} %copy-done.44), kind=kOutput, calls=%fused_computation.47 | convolution fusion | flops 44631168 | bytes 3475456 | tf_op jit(solution)/shard_map/hqk,qhd->khd/dot_general | solution.py:114
  125.0 2.6 convolution_bitcast_fusion.1
  127.6 1.5 fusion.15
  131.3 5.2 fusion.49
  136.6 5.9 convolution_bitcast_fusion.5
  142.5 1.8 convolution_bitcast_fusion.2
  146.5 1.4 collective-permute-start.15
  147.9 1.3 collective-permute-start.13
  149.2 1.3 collective-permute-start.14
  150.5 1.3 collective-permute-start.12
  151.8 1.3 collective-permute-start.11
  153.7 7.4 %collective-permute-done.15 = f32[128,768]{0,1:T(8,128)S(1)} collective-permute-done((f32[128,768]{0,1:T(8,128)S(1)}, f32[128,768]{0,1:T(8,128)S(1)}, u32[]{:S(2)}, u32[]{:S(2)}) %collective-permute-start.15) | collective-permute-done | bytes 393248 | tf_op jit(solution)/shard_map/ppermute | solution.py:17
  161.1 1.3 collective-permute-start.9
  162.4 19.3 %collective-permute-done.13 = f32[128,768]{0,1:T(8,128)S(1)} collective-permute-done((f32[128,768]{0,1:T(8,128)S(1)}, f32[128,768]{0,1:T(8,128)S(1)}, u32[]{:S(2)}, u32[]{:S(2)}) %collective-permute-start.13) | collective-permute-done | bytes 393248 | tf_op jit(solution)/shard_map/ppermute | solution.py:17
  181.7 1.3 collective-permute-start.10
  183.0 8.8 %collective-permute-done.14 = f32[128,768]{0,1:T(8,128)S(1)} collective-permute-done((f32[128,768]{0,1:T(8,128)S(1)}, f32[128,768]{0,1:T(8,128)S(1)}, u32[]{:S(2)}, u32[]{:S(2)}) %collective-permute-start.14) | collective-permute-done | bytes 393248 | tf_op jit(solution)/shard_map/ppermute | solution.py:17
  191.8 1.3 collective-permute-start.8
  193.7 36.3 %collective-permute-done.9 = f32[128,768]{0,1:T(8,128)S(1)} collective-permute-done((f32[128,768]{0,1:T(8,128)S(1)}, f32[128,768]{0,1:T(8,128)S(1)}, u32[]{:S(2)}, u32[]{:S(2)}) %collective-permute-start.9) | collective-permute-done | bytes 393248 | tf_op jit(solution)/shard_map/ppermute | solution.py:17
  231.4 2.5 pad_maximum_fusion
  236.6 279.6 %reduce-scatter.2.cloned.1.call-done = bf16[96,768]{1,0:T(8,128)(2,1)} async-done(((bf16[3072,768]{1,0:T(8,128)(2,1)}), bf16[96,768]{1,0:T(8,128)(2,1)}) %reduce-scatter.2.cloned.1.call-update) | async-done | bytes 147472 | tf_op jit(solution)/shard_map/reduce_scatter | solution.py:217
  516.9 65.5 %all-reduce.2.cloned.1.call-done = bf16[96,768]{1,0:T(8,128)(2,1)} async-done(((bf16[96,768]{1,0:T(8,128)(2,1)}), bf16[96,768]{1,0:T(8,128)(2,1)}) %all-reduce.2.cloned.1.call-update) | async-done | bytes 147472 | tf_op jit(solution)/shard_map/psum | solution.py:218
  582.5 1.6 convert_element_type.109
  (159 shorter events, 31.2 us)
Async XLA Ops:
  7.2 2.3 copy-start
  7.2 508.9 %reduce-scatter.2.cloned.1.call-start = ((), (), s32[]{:S(2)}) async-start(), calls=%async_computation.1 | async-start | bytes 4866048 | tf_op jit(solution)/shard_map/reduce_scatter | solution.py:217
  7.2 22.0 %copy-start.1 = (bf16[768,768]{1,0:T(8,128)(2,1)S(1)}, bf16[768,768]{1,0:T(8,128)(2,1)}, u32[]{:S(2)}) copy-start(bf16[768,768]{1,0:T(8,128)(2,1)} %param.11) | copy-start | bytes 3538948
  10.5 59.0 %collective-permute-start.7 = (bf16[128,768]{1,0:T(8,128)(2,1)}, bf16[128,768]{1,0:T(8,128)(2,1)}, u32[]{:S(2)}, u32[]{:S(2)}) collective-permute-start(bf16[128,768]{1,0:T(8,128)(2,1)} %convolution_convert_fusion.4), channel_id=1, source_target_pairs={{0,1},{1,2},{2,3},{3,4},{4,5},{5,6},{6,7},{7,8},{8,9},{9,10},{10,1... | collective-permute-start | bytes 589832 | tf_op jit(solution)/shard_map/ppermute | solution.py:17
  15.5 44.4 %collective-permute-start.6 = (bf16[128,768]{1,0:T(8,128)(2,1)}, bf16[128,768]{1,0:T(8,128)(2,1)}, u32[]{:S(2)}, u32[]{:S(2)}) collective-permute-start(bf16[128,768]{1,0:T(8,128)(2,1)} %convolution_convert_fusion.4), channel_id=1, source_target_pairs={{0,2},{1,3},{2,4},{3,5},{4,6},{5,7},{6,8},{7,9},{8,10},{9,11},{10,... | collective-permute-start | bytes 589832 | tf_op jit(solution)/shard_map/ppermute | solution.py:17
  20.4 35.9 %collective-permute-start.5 = (bf16[128,768]{1,0:T(8,128)(2,1)}, bf16[128,768]{1,0:T(8,128)(2,1)}, u32[]{:S(2)}, u32[]{:S(2)}) collective-permute-start(bf16[128,768]{1,0:T(8,128)(2,1)} %convolution_convert_fusion.4), channel_id=1, source_target_pairs={{0,3},{1,4},{2,5},{3,6},{4,7},{5,8},{6,9},{7,10},{8,11},{9,12},{10... | collective-permute-start | bytes 589832 | tf_op jit(solution)/shard_map/ppermute | solution.py:17
  26.1 18.6 %collective-permute-start.4 = (bf16[128,768]{1,0:T(8,128)(2,1)}, bf16[128,768]{1,0:T(8,128)(2,1)}, u32[]{:S(2)}, u32[]{:S(2)}) collective-permute-start(bf16[128,768]{1,0:T(8,128)(2,1)} %convolution_convert_fusion.4), channel_id=1, source_target_pairs={{0,4},{1,5},{2,6},{3,7},{4,8},{5,9},{6,10},{7,11},{8,12},{9,13},{1... | collective-permute-start | bytes 589832 | tf_op jit(solution)/shard_map/ppermute | solution.py:17
  31.1 7.3 %copy-start.10 = (bf16[1,128,768]{2,1,0:T(8,128)(2,1)S(1)}, bf16[1,128,768]{2,1,0:T(8,128)(2,1)}, u32[]{:S(2)}) copy-start(bf16[1,128,768]{2,1,0:T(8,128)(2,1)} %param.9) | copy-start | bytes 589828
  32.8 55.0 %collective-permute-start.3 = (bf16[128,768]{0,1:T(8,128)(2,1)}, bf16[128,768]{0,1:T(8,128)(2,1)}, u32[]{:S(2)}, u32[]{:S(2)}) collective-permute-start(bf16[128,768]{0,1:T(8,128)(2,1)} %bitcast.2), channel_id=1, source_target_pairs={{0,1},{1,2},{2,3},{3,4},{4,5},{5,6},{6,7},{7,8},{8,9},{9,10},{10,1... | collective-permute-start | bytes 589832 | tf_op jit(solution)/shard_map/ppermute | solution.py:17
  44.7 40.6 %collective-permute-start.2 = (bf16[128,768]{0,1:T(8,128)(2,1)}, bf16[128,768]{0,1:T(8,128)(2,1)}, u32[]{:S(2)}, u32[]{:S(2)}) collective-permute-start(bf16[128,768]{0,1:T(8,128)(2,1)} %bitcast.2), channel_id=1, source_target_pairs={{0,2},{1,3},{2,4},{3,5},{4,6},{5,7},{6,8},{7,9},{8,10},{9,11},{10,... | collective-permute-start | bytes 589832 | tf_op jit(solution)/shard_map/ppermute | solution.py:17
  56.3 26.5 %collective-permute-start.1 = (bf16[128,768]{0,1:T(8,128)(2,1)}, bf16[128,768]{0,1:T(8,128)(2,1)}, u32[]{:S(2)}, u32[]{:S(2)}) collective-permute-start(bf16[128,768]{0,1:T(8,128)(2,1)} %bitcast.2), channel_id=1, source_target_pairs={{0,3},{1,4},{2,5},{3,6},{4,7},{5,8},{6,9},{7,10},{8,11},{9,12},{10... | collective-permute-start | bytes 589832 | tf_op jit(solution)/shard_map/ppermute | solution.py:17
  59.9 19.5 %collective-permute-start = (bf16[128,768]{0,1:T(8,128)(2,1)}, bf16[128,768]{0,1:T(8,128)(2,1)}, u32[]{:S(2)}, u32[]{:S(2)}) collective-permute-start(bf16[128,768]{0,1:T(8,128)(2,1)} %bitcast.2), channel_id=1, source_target_pairs={{0,4},{1,5},{2,6},{3,7},{4,8},{5,9},{6,10},{7,11},{8,12},{9,13},{1... | collective-permute-start | bytes 589832 | tf_op jit(solution)/shard_map/ppermute | solution.py:17
  75.0 8.8 %copy-start.4 = (bf16[640,768]{0,1:T(8,128)(2,1)S(1)}, bf16[640,768]{0,1:T(8,128)(2,1)}, u32[]{:S(2)}) copy-start(bf16[640,768]{0,1:T(8,128)(2,1)} %copy.23) | copy-start | bytes 2949124
  86.3 4.4 copy-start.23
  86.3 4.4 copy-start.27
  86.3 4.4 copy-start.35
  86.3 4.4 copy-start.47
  106.2 2.6 copy-start.24
  106.2 2.6 copy-start.28
  106.2 2.6 copy-start.36
  106.2 2.6 copy-start.46
  125.0 2.6 copy-start.25
  125.0 2.6 copy-start.29
  125.0 2.6 copy-start.37
  125.0 2.6 copy-start.45
  129.1 1.7 copy-start.6
  131.3 5.2 copy-start.26
  131.3 5.2 copy-start.30
  131.3 5.2 copy-start.42
  142.5 1.8 copy-start.13
  142.5 1.8 copy-start.15
  142.5 1.9 copy-start.16
  146.2 6.9 %copy-start.31 = (bf16[128,4,64]{0,2,1:T(8,128)(2,1)S(1)}, bf16[128,4,64]{0,2,1:T(8,128)(2,1)}, u32[]{:S(2)}) copy-start(bf16[128,4,64]{0,2,1:T(8,128)(2,1)} %fusion.60) | copy-start | bytes 196612
  146.2 6.9 %copy-start.32 = (bf16[128,4,64]{0,2,1:T(8,128)(2,1)S(1)}, bf16[128,4,64]{0,2,1:T(8,128)(2,1)}, u32[]{:S(2)}) copy-start(bf16[128,4,64]{0,2,1:T(8,128)(2,1)} %fusion.59) | copy-start | bytes 196612
  146.2 7.0 %copy-start.21 = (f32[128,4,64]{0,2,1:T(8,128)S(1)}, f32[128,4,64]{0,2,1:T(8,128)}, u32[]{:S(2)}) copy-start(f32[128,4,64]{0,2,1:T(8,128)} %fusion.55) | copy-start | bytes 393220
  146.2 6.9 %copy-start.22 = (f32[128,4,64]{0,2,1:T(8,128)S(1)}, f32[128,4,64]{0,2,1:T(8,128)}, u32[]{:S(2)}) copy-start(f32[128,4,64]{0,2,1:T(8,128)} %fusion.52) | copy-start | bytes 393220
  146.4 6.8 %copy-start.11 = (bf16[1,128,768]{2,1,0:T(8,128)(2,1)S(1)}, bf16[1,128,768]{2,1,0:T(8,128)(2,1)}, u32[]{:S(2)}) copy-start(bf16[1,128,768]{2,1,0:T(8,128)(2,1)} %param.9) | copy-start | bytes 589828
  146.5 14.6 %collective-permute-start.15 = (f32[128,768]{0,1:T(8,128)S(1)}, f32[128,768]{0,1:T(8,128)S(1)}, u32[]{:S(2)}, u32[]{:S(2)}) collective-permute-start(f32[128,768]{0,1:T(8,128)S(1)} %bitcast.119), channel_id=1, source_target_pairs={{4,0},{5,1},{6,2},{7,3},{8,4},{9,5},{10,6},{11,7},{12,8},{13,9},{1... | collective-permute-start | bytes 1179656 | tf_op jit(solution)/shard_map/ppermute | solution.py:17
  147.9 33.8 %collective-permute-start.13 = (f32[128,768]{0,1:T(8,128)S(1)}, f32[128,768]{0,1:T(8,128)S(1)}, u32[]{:S(2)}, u32[]{:S(2)}) collective-permute-start(f32[128,768]{0,1:T(8,128)S(1)} %bitcast.118), channel_id=1, source_target_pairs={{2,0},{3,1},{4,2},{5,3},{6,4},{7,5},{8,6},{9,7},{10,8},{11,9},{12,... | collective-permute-start | bytes 1179656 | tf_op jit(solution)/shard_map/ppermute | solution.py:17
  149.2 42.6 %collective-permute-start.14 = (f32[128,768]{0,1:T(8,128)S(1)}, f32[128,768]{0,1:T(8,128)S(1)}, u32[]{:S(2)}, u32[]{:S(2)}) collective-permute-start(f32[128,768]{0,1:T(8,128)S(1)} %bitcast.117), channel_id=1, source_target_pairs={{3,0},{4,1},{5,2},{6,3},{7,4},{8,5},{9,6},{10,7},{11,8},{12,9},{13... | collective-permute-start | bytes 1179656 | tf_op jit(solution)/shard_map/ppermute | solution.py:17
  150.5 42.6 %collective-permute-start.12 = (f32[128,768]{0,1:T(8,128)S(1)}, f32[128,768]{0,1:T(8,128)S(1)}, u32[]{:S(2)}, u32[]{:S(2)}) collective-permute-start(f32[128,768]{0,1:T(8,128)S(1)} %bitcast.116), channel_id=1, source_target_pairs={{1,0},{2,1},{3,2},{4,3},{5,4},{6,5},{7,6},{8,7},{9,8},{10,9},{11,1... | collective-permute-start | bytes 1179656 | tf_op jit(solution)/shard_map/ppermute | solution.py:17
  151.8 42.0 %collective-permute-start.11 = (f32[128,768]{0,1:T(8,128)S(1)}, f32[128,768]{0,1:T(8,128)S(1)}, u32[]{:S(2)}, u32[]{:S(2)}) collective-permute-start(f32[128,768]{0,1:T(8,128)S(1)} %bitcast.115), channel_id=1, source_target_pairs={{4,0},{5,1},{6,2},{7,3},{8,4},{9,5},{10,6},{11,7},{12,8},{13,9},{1... | collective-permute-start | bytes 1179656 | tf_op jit(solution)/shard_map/ppermute | solution.py:17
  161.1 69.0 %collective-permute-start.9 = (f32[128,768]{0,1:T(8,128)S(1)}, f32[128,768]{0,1:T(8,128)S(1)}, u32[]{:S(2)}, u32[]{:S(2)}) collective-permute-start(f32[128,768]{0,1:T(8,128)S(1)} %bitcast.114), channel_id=1, source_target_pairs={{2,0},{3,1},{4,2},{5,3},{6,4},{7,5},{8,6},{9,7},{10,8},{11,9},{12,... | collective-permute-start | bytes 1179656 | tf_op jit(solution)/shard_map/ppermute | solution.py:17
  181.7 48.4 %collective-permute-start.10 = (f32[128,768]{0,1:T(8,128)S(1)}, f32[128,768]{0,1:T(8,128)S(1)}, u32[]{:S(2)}, u32[]{:S(2)}) collective-permute-start(f32[128,768]{0,1:T(8,128)S(1)} %bitcast.113), channel_id=1, source_target_pairs={{3,0},{4,1},{5,2},{6,3},{7,4},{8,5},{9,6},{10,7},{11,8},{12,9},{13... | collective-permute-start | bytes 1179656 | tf_op jit(solution)/shard_map/ppermute | solution.py:17
  191.8 38.3 %collective-permute-start.8 = (f32[128,768]{0,1:T(8,128)S(1)}, f32[128,768]{0,1:T(8,128)S(1)}, u32[]{:S(2)}, u32[]{:S(2)}) collective-permute-start(f32[128,768]{0,1:T(8,128)S(1)} %bitcast.112), channel_id=1, source_target_pairs={{1,0},{2,1},{3,2},{4,3},{5,4},{6,5},{7,6},{8,7},{9,8},{10,9},{11,1... | collective-permute-start | bytes 1179656 | tf_op jit(solution)/shard_map/ppermute | solution.py:17
  193.7 36.5 %copy-start.18 = (f32[128,32]{0,1:T(8,128)S(1)}, f32[128,32]{0,1:T(8,128)}, u32[]{:S(2)}) copy-start(f32[128,32]{0,1:T(8,128)} %copy-done.17) | copy-start | bytes 49156
  193.7 36.5 %copy-start.20 = (f32[128,32]{0,1:T(8,128)S(1)}, f32[128,32]{0,1:T(8,128)}, u32[]{:S(2)}) copy-start(f32[128,32]{0,1:T(8,128)} %copy-done.19) | copy-start | bytes 49156
  233.9 348.6 %all-reduce.2.cloned.1.call-start = ((), (), s32[]{:S(2)}) async-start(), calls=%async_computation.2 | async-start | bytes 294912 | tf_op jit(solution)/shard_map/psum | solution.py:218
  (18 other events, 19.6 us)
Sparse Core Ops, SparseCore 0:
  234.0 282.0 reduce-scatter.1
  518.4 63.9 all-reduce.1
where the time goes:
time: 593 us; the launch traced here: 591 us
  waiting for transfers between devices  421 us (71%)
  matrix products  63.4 us (11%)
  starting transfers between devices  53.4 us (9%)
  local copies, waits for them, and re-layouts  26.3 us (4%)
  between operations  14.8 us (2%)
  other arithmetic  11.7 us (2%)
    reduce_scatter x1, waiting for transfers between devices, on_device(): lax.psum_scatter(term.astype(jnp.bfloat16), 'seq', scatter_dimension=0, t...  280 us
    ppermute x16, waiting for transfers between devices, shifted(): return lax.ppermute(block, axis, route)  76.3 us
    psum x1, waiting for transfers between devices, on_device(): weight_grads = lax.psum(shares, 'dp').astype(jnp.float32)  65.5 us
    ppermute x16, starting transfers between devices, shifted(): return lax.ppermute(block, axis, route)  53.3 us
    unnamed x104, local copies, waits for them, and re-layouts  18.4 us
    dot_general x3, matrix products, head_group(): jnp.einsum('hqk,qhd->khd', grad_scores, query_heads, preferred_element_ty...  18.1 us
    dot_general x3, matrix products, head_group(): jnp.einsum('hqk,khd->qhd', grad_scores, key_heads, preferred_element_type...  17 us
  transfers between devices with their start and end apart: 18, of which 7 were waited for; matrix products, arithmetic and copies ran while one was open for 5% of the time, Pallas kernels for 0%

commit v1 on v0

v1 whole, which is shorter than its diff:
```python
import functools

import jax
import jax.numpy as jnp
import numpy as np
from jax import lax
from jax.experimental import pallas as pl
from jax.experimental.pallas import tpu as pltpu
from jax.sharding import PartitionSpec as P

D = 768
HEADS = 12
HEAD_DIM = 64
VOCAB = 256
WINDOW = 512
EPSILON = 1e-05
B = 128
SEQ_DEVS = 32
REACH = WINDOW // B
SPAN = (REACH + 1) * B
PAIRS = D // B
MESH = pl.DeviceIdType.MESH
BF = jnp.bfloat16
F32 = jnp.float32
TERM_ROWS = 3 * VOCAB + D


def rope_tables():
    frequency = 10000.0 ** (-2.0 * np.arange(HEAD_DIM // 2) / HEAD_DIM)
    lane_frequency = np.tile(frequency, 4)[None, :]
    inside = np.arange(B)[:, None] * lane_frequency
    blocks = (np.arange(SEQ_DEVS) * B)[:, None] * lane_frequency
    return [
        np.asarray(part, np.float32)
        for part in (np.cos(inside), np.sin(inside), np.cos(blocks), np.sin(blocks))
    ]


def nn(a, b):
    return lax.dot_general(a, b, (((1,), (0,)), ((), ())), preferred_element_type=F32)


def nt(a, b):
    return lax.dot_general(a, b, (((1,), (1,)), ((), ())), preferred_element_type=F32)


def tn(a, b):
    return lax.dot_general(a, b, (((0,), (0,)), ((), ())), preferred_element_type=F32)


def swap_halves(x):
    lane = lax.broadcasted_iota(jnp.int32, x.shape, 1)
    first = (lane // (HEAD_DIM // 2)) % 2 == 0
    return jnp.where(first, pltpu.roll(x, B - HEAD_DIM // 2, 1), pltpu.roll(x, HEAD_DIM // 2, 1))


def rope(x, cosine, sine):
    return x * cosine + swap_halves(x) * sine


def unrope(x, cosine, sine):
    return x * cosine - swap_halves(x) * sine


def kernel(
    ids_ref, cot_hbm, table_hbm, wq_hbm, wk_hbm, wv_hbm, wo_hbm, window_ref, cr_ref, sr_ref, cb_ref, sb_ref,
    gin_ref, wg_ref,
    ids_all, cot_all, table, wq, wk, wv, wo, ntab, normed, emb, cosv, sinv,
    keys, values, query, gatt, att, gq, gk, gv, onehot_t, statc, stats,
    probs_s, ds_s,
    term, r1, s1, r2, s2, r3, a4, r4, r5,
    load_sem, ids_send, ids_recv, cot_send, cot_recv, st_send, st_recv,
    p1_send, p1_recv, p2_send, p2_recv, p3_send, p3_recv, p4_send, p4_recv, p5_send, p5_recv,
):
    dp = lax.axis_index("dp")
    sq = lax.axis_index("seq")
    x, z = sq // 8, sq % 8
    y, c = dp // 2, dp % 2
    base = sq * B

    loads = [
        pltpu.make_async_copy(src, dst, load_sem.at[i])
        for i, (src, dst) in enumerate(
            [(cot_hbm, cot_all.at[0]), (table_hbm, table), (wk_hbm, wk), (wv_hbm, wv), (wq_hbm, wq), (wo_hbm, wo)]
        )
    ]
    for load in loads:
        load.start()

    def at(new_dp, new_sq):
        return (new_dp, new_sq)

    def seq_of(new_x, new_z):
        return new_x * 8 + new_z

    def shift(distance):
        return lax.rem(sq + distance + SEQ_DEVS, SEQ_DEVS)

    def other_dp(step):
        return lax.rem(dp + step, 8)

    def other_y(step):
        return lax.rem(y + step, 4)

    def other_x(step):
        return lax.rem(x + step, 4)

    def other_z(step):
        return lax.rem(z + step, 8)

    barrier = pltpu.get_barrier_semaphore()
    partners = [at(dp, shift(d)) for d in (1, 2, 3, 4, -1, -2, -3, -4)]
    partners += [at(other_dp(d), sq) for d in range(1, 8)]
    partners += [at(dp, seq_of(other_x(d), z)) for d in range(1, 4)]
    partners += [at(dp, seq_of(x, other_z(d))) for d in range(1, 8)]
    for partner in partners:
        pl.semaphore_signal(barrier, inc=1, device_id=partner, device_id_type=MESH)

    lane_row = lax.broadcasted_iota(jnp.int32, (1, B), 1)
    sign = jnp.where((lane_row // (HEAD_DIM // 2)) % 2 == 0, -1.0, 1.0)

    def rope_block(i, carry):
        block = lax.rem(sq + i - REACH + SEQ_DEVS, SEQ_DEVS)
        cb = cb_ref[pl.ds(block, 1), :]
        sb = sb_ref[pl.ds(block, 1), :]
        rows = pl.ds(pl.multiple_of(i * B, B), B)
        cosv[rows, :] = cr_ref[...] * cb - sr_ref[...] * sb
        sinv[rows, :] = (sr_ref[...] * cb + cr_ref[...] * sb) * sign
        return carry

    lax.fori_loop(0, 2 * REACH + 1, rope_block, 0)

    loads[1].wait()
    rows_f = table[...].astype(F32)
    table_inv = lax.rsqrt(jnp.mean(rows_f * rows_f, axis=1, keepdims=True) + EPSILON)
    ntab[...] = (rows_f * table_inv).astype(BF)

    loads[0].wait()
    pl.semaphore_wait(barrier, len(partners))

    def remote(src, dst, send, recv, device):
        return pltpu.make_async_remote_copy(
            src_ref=src, dst_ref=dst, send_sem=send, recv_sem=recv, device_id=device, device_id_type=MESH
        )

    id_copies = []
    for i, d in enumerate((1, 2, 3, 4, -1, -2, -3, -4)):
        id_copies.append(remote(ids_ref, ids_all.at[d + REACH], ids_send.at[i], ids_recv.at[i], at(dp, shift(-d))))

    def relay(step):
        return remote(
            cot_all.at[step], cot_all.at[step + 1], cot_send.at[step], cot_recv.at[step], at(dp, shift(-1))
        )

    relays = [relay(step) for step in range(REACH)]
    for copy in id_copies:
        copy.start()
    relays[0].start()
    ids_all[REACH] = ids_ref[...]
    for copy in id_copies:
        copy.wait_recv()

    token = lax.broadcasted_iota(jnp.int32, (VOCAB, B), 0)
    onehot_t[...] = (token == ids_ref[...]).astype(BF)
    emb[...] = tn(onehot_t[...], table[...])

    def embed_block(i, carry):
        rows = pl.ds(pl.multiple_of(i * B, B), B)
        hot = (token == ids_all[i]).astype(BF)
        normed[rows, :] = tn(hot, ntab[...]).astype(BF)
        return carry

    lax.fori_loop(0, 2 * REACH + 1, embed_block, 0)

    def project(first, w, out, rotated, scale):
        def slab(j, carry):
            lanes = pl.ds(pl.multiple_of(j * B, B), B)
            got = nn(normed[pl.ds(first, SPAN), :], w[:, lanes])
            if rotated:
                got = rope(got, cosv[pl.ds(first, SPAN), :], sinv[pl.ds(first, SPAN), :])
            out[:, lanes] = (got.astype(BF) * scale).astype(BF) if scale != 1.0 else got.astype(BF)
            return carry

        lax.fori_loop(0, PAIRS, slab, 0)

    loads[2].wait()
    project(0, wk, keys, True, 1.0)
    loads[3].wait()
    project(0, wv, values, False, 1.0)
    loads[4].wait()
    project(REACH * B, wq, query, True, HEAD_DIM ** (-0.5))
    loads[5].wait()
    gatt[pl.ds(0, B), :] = nt(cot_all[0], wo[...]).astype(BF)

    relays[0].wait_recv()
    relays[1].start()

    lane_one = lax.broadcasted_iota(jnp.int32, (1, B), 1)
    left = (lane_one < HEAD_DIM).astype(BF)
    right = (lane_one >= HEAD_DIM).astype(BF)

    def stacked(a):
        return jnp.concatenate([a * left, a * right], axis=0)

    def picked(a):
        return jnp.where(lane_one < HEAD_DIM, a[:B], a[B:])

    own_cos = cosv[pl.ds(REACH * B, B), :]
    own_sin = sinv[pl.ds(REACH * B, B), :]
    statc[...] = jnp.zeros_like(statc)

    def pass_one(p, carry):
        lanes = pl.ds(pl.multiple_of(p * B, B), B)
        k, v = keys[:, lanes], values[:, lanes]
        scores = nt(stacked(query[pl.ds(0, B), lanes]), k)
        row = lax.broadcasted_iota(jnp.int32, (2 * B, SPAN), 0)
        col = lax.broadcasted_iota(jnp.int32, (2 * B, SPAN), 1)
        dist = row % B + WINDOW - col
        row_one = lax.broadcasted_iota(jnp.int32, (2 * B, 1), 0)
        width = jnp.where(row_one < B, window_ref[2 * p], window_ref[2 * p + 1])
        allowed = (dist >= 0) & (dist < width) & (col >= WINDOW - base)
        masked = jnp.where(allowed, scores, -1e30)
        top = jnp.max(masked, axis=1, keepdims=True)
        weights = jnp.exp(masked - top)
        scale = 1.0 / jnp.sum(weights, axis=1, keepdims=True)
        probs = weights * scale
        grad_probs = nt(stacked(gatt[pl.ds(0, B), lanes]), v)
        row_term = jnp.sum(probs * grad_probs, axis=1, keepdims=True)
        ds = (probs * (grad_probs - row_term)).astype(BF)
        att[:, lanes] = picked(nn(probs.astype(BF), v)).astype(BF)
        grad_query = picked(nn(ds, k)) * HEAD_DIM ** (-0.5)
        gq[:, lanes] = unrope(grad_query, own_cos, own_sin).astype(BF)
        held = statc[...]
        for j, stat in enumerate((top, scale, row_term)):
            held = jnp.where(lane_one == 16 * j + 2 * p, stat[:B], held)
            held = jnp.where(lane_one == 16 * j + 2 * p + 1, stat[B:], held)
        statc[...] = held
        return carry

    lax.fori_loop(0, PAIRS, pass_one, 0)

    relays[1].wait_recv()
    relays[2].start()

    stats[0] = statc[...].T[: 3 * 16]
    stat_copies = []
    for d in range(1, REACH + 1):
        stat_copies.append(
            remote(stats.at[0], stats.at[d], st_send.at[d - 1], st_recv.at[d - 1], at(dp, shift(-d)))
        )
    for copy in stat_copies:
        copy.start()

    relays[2].wait_recv()
    relays[3].start()
    for d in range(1, REACH):
        gatt[pl.ds(d * B, B), :] = nt(cot_all[d], wo[...]).astype(BF)
    relays[3].wait_recv()
    gatt[pl.ds(REACH * B, B), :] = nt(cot_all[REACH], wo[...]).astype(BF)
    for copy in stat_copies:
        copy.wait_recv()

    def pass_two(p, carry):
        lanes = pl.ds(pl.multiple_of(p * B, B), B)
        k2 = stacked(keys[pl.ds(REACH * B, B), lanes])
        v2 = stacked(values[pl.ds(REACH * B, B), lanes])
        row_one = lax.broadcasted_iota(jnp.int32, (2 * B, 1), 0)
        width = jnp.where(row_one < B, window_ref[2 * p], window_ref[2 * p + 1])
        row = lax.broadcasted_iota(jnp.int32, (2 * B, B), 0) % B
        col = lax.broadcasted_iota(jnp.int32, (2 * B, B), 1)
        for d in range(REACH + 1):
            q, g = query[pl.ds(d * B, B), lanes], gatt[pl.ds(d * B, B), lanes]
            dist = col + d * B - row
            allowed = (dist >= 0) & (dist < width) & (col + d * B < SEQ_DEVS * B - base)

            def spread(j):
                a = jnp.broadcast_to(stats[d, pl.ds(16 * j + 2 * p, 1), :], (B, B))
                b = jnp.broadcast_to(stats[d, pl.ds(16 * j + 2 * p + 1, 1), :], (B, B))
                return jnp.concatenate([a, b], axis=0)

            masked = jnp.where(allowed, nt(k2, q), -1e30)
            weights = jnp.exp(jnp.where(allowed, masked - spread(0), -1e30))
            probs = weights * spread(1)
            ds = probs * (nt(v2, g) - spread(2))
            probs_s[:, pl.ds(d * B, B)] = probs.astype(BF)
            ds_s[:, pl.ds(d * B, B)] = ds.astype(BF)
        grad_value = picked(nn(probs_s[...], gatt[:, lanes]))
        grad_key = picked(nn(ds_s[...], query[:, lanes]))
        gv[:, lanes] = grad_value.astype(BF)
        gk[:, lanes] = unrope(grad_key, own_cos, own_sin).astype(BF)
        return carry

    lax.fori_loop(0, PAIRS, pass_two, 0)

    att_t = att[...].T

    def terms(p, carry):
        lanes = pl.ds(pl.multiple_of(p * B, B), B)
        core, row = p % 2, p // 2
        hot = onehot_t[...]
        term[core, row, pl.ds(0, VOCAB), :] = nn(hot, gq[:, lanes]).astype(BF)
        term[core, row, pl.ds(VOCAB, VOCAB), :] = nn(hot, gk[:, lanes]).astype(BF)
        term[core, row, pl.ds(2 * VOCAB, VOCAB), :] = nn(hot, gv[:, lanes]).astype(BF)
        term[core, row, pl.ds(3 * VOCAB, D), :] = nn(att_t, cot_all[0, :, lanes]).astype(BF)
        return carry

    lax.fori_loop(0, PAIRS, terms, 0)

    p1 = remote(term.at[1 - c], r1, p1_send.at[0], p1_recv.at[0], at(y * 2 + 1 - c, sq))
    p1.start()

    grad_normed = nt(gq[...], wq[...]) + nt(gk[...], wk[...]) + nt(gv[...], wv[...])
    own = emb[...]
    inv = lax.rsqrt(jnp.mean(own * own, axis=1, keepdims=True) + EPSILON)
    scaled = own * inv
    gin_ref[...] = (
        inv * (grad_normed - scaled * jnp.mean(grad_normed * scaled, axis=1, keepdims=True))
    ).astype(BF)

    p1.wait_recv()
    for row in range(3):
        s1[row] = (term[c, row].astype(F32) + r1[row].astype(F32)).astype(BF)

    def p2(step):
        return remote(
            s1.at[lax.min(other_y(step), 2)], r2.at[step - 1], p2_send.at[step - 1], p2_recv.at[step - 1],
            at(other_y(step) * 2 + c, sq),
        )

    for step in range(1, 4):
        @pl.when(other_y(step) < 3)
        def _():
            p2(step).start()

    def p3_token(step, target):
        return remote(
            s2.at[pl.ds(pl.multiple_of(target * VOCAB, VOCAB), VOCAB)], r3.at[step - 1, pl.ds(0, VOCAB)],
            p3_send.at[step - 1], p3_recv.at[step - 1], at(dp, seq_of(target, z)),
        )

    def p3_out(step):
        return remote(
            s2.at[pl.ds(3 * VOCAB, D)], r3.at[step - 1],
            p3_send.at[step - 1], p3_recv.at[step - 1], at(dp, seq_of(3, z)),
        )

    def p4(step):
        return remote(
            a4.at[other_z(step)], r4.at[step - 1], p4_send.at[step - 1], p4_recv.at[step - 1],
            at(dp, seq_of(x, other_z(step))),
        )

    @pl.when(y < 3)
    def _():
        for step in range(1, 4):
            p2(step).wait_recv()
        total = s1[lax.min(y, 2)].astype(F32)
        for step in range(3):
            total += r2[step].astype(F32)
        s2[...] = total.astype(BF)

        for step in range(1, 4):
            @pl.when(other_x(step) < 3)
            def _():
                p3_token(step, lax.min(other_x(step), 2)).start()

            @pl.when(other_x(step) == 3)
            def _():
                p3_out(step).start()

        @pl.when(x < 3)
        def _():
            for step in range(1, 4):
                p3_token(step, lax.min(x, 2)).wait_recv()
            total = s2[pl.ds(pl.multiple_of(lax.min(x, 2) * VOCAB, VOCAB), VOCAB), :].astype(F32)
            for step in range(3):
                total += r3[step, pl.ds(0, VOCAB), :].astype(F32)
            a4[...] = tn(ntab[...], total.astype(BF)).astype(BF).reshape(8, D // 8, B)

        @pl.when(x == 3)
        def _():
            for step in range(1, 4):
                p3_out(step).wait_recv()
            total = s2[pl.ds(3 * VOCAB, D), :].astype(F32)
            for step in range(3):
                total += r3[step].astype(F32)
            a4[...] = total.astype(BF).reshape(8, D // 8, B)

        for step in range(1, 8):
            p4(step).start()
        for step in range(1, 8):
            p4(step).wait_recv()
        total = a4[z].astype(F32)
        for step in range(7):
            total += r4[step].astype(F32)
        r5[dp] = total.astype(BF)

    def p5(step):
        mine = lax.min(dp, 5)
        return remote(r5.at[mine], r5.at[mine], p5_send.at[step - 1], p5_recv.at[step - 1], at(other_dp(step), sq))

    def p5_from(step):
        owner = lax.rem(dp + 8 - step, 8)
        slot = lax.min(owner, 5)
        return owner, remote(
            r5.at[slot], r5.at[slot], p5_send.at[step - 1], p5_recv.at[step - 1], at(other_dp(step), sq)
        )

    @pl.when(dp < 6)
    def _():
        for step in range(1, 8):
            p5(step).start()

    for step in range(1, 8):
        owner, copy = p5_from(step)

        @pl.when(owner < 6)
        def _():
            copy.wait_recv()

    for p in range(PAIRS):
        wg_ref[:, pl.ds(p * B, B)] = r5[p].astype(F32)

    for copy in id_copies + relays + stat_copies + [p1]:
        copy.wait_send()
    for step in range(1, 4):
        @pl.when(other_y(step) < 3)
        def _():
            p2(step).wait_send()

    @pl.when(y < 3)
    def _():
        for step in range(1, 4):
            @pl.when(other_x(step) < 3)
            def _():
                p3_token(step, lax.min(other_x(step), 2)).wait_send()

            @pl.when(other_x(step) == 3)
            def _():
                p3_out(step).wait_send()
        for step in range(1, 8):
            p4(step).wait_send()
            p5(step).wait_send()


def on_device(token_ids, cotangent, table, w_query, w_key, w_value, w_out, window):
    tables = [jnp.asarray(part) for part in rope_tables()]
    vmem = pl.BlockSpec(memory_space=pltpu.VMEM)
    hbm = pl.BlockSpec(memory_space=pl.ANY)
    smem = pl.BlockSpec(memory_space=pltpu.SMEM)
    dma = pltpu.SemaphoreType.DMA
    grad_input, weight_grads = pl.pallas_call(
        kernel,
        out_shape=(
            jax.ShapeDtypeStruct((B, D), BF),
            jax.ShapeDtypeStruct((D // 8, D), F32),
        ),
        in_specs=[vmem] + [hbm] * 6 + [smem] + [vmem] * 4,
        out_specs=(vmem, vmem),
        scratch_shapes=[
            pltpu.VMEM((2 * REACH + 1, 1, B), jnp.int32),
            pltpu.VMEM((REACH + 1, B, D), BF),
            pltpu.VMEM((VOCAB, D), BF),
            pltpu.VMEM((D, D), BF),
            pltpu.VMEM((D, D), BF),
            pltpu.VMEM((D, D), BF),
            pltpu.VMEM((D, D), BF),
            pltpu.VMEM((VOCAB, D), BF),
            pltpu.VMEM(((2 * REACH + 1) * B, D), BF),
            pltpu.VMEM((B, D), F32),
            pltpu.VMEM(((2 * REACH + 1) * B, B), F32),
            pltpu.VMEM(((2 * REACH + 1) * B, B), F32),
            pltpu.VMEM((SPAN, D), BF),
            pltpu.VMEM((SPAN, D), BF),
            pltpu.VMEM((SPAN, D), BF),
            pltpu.VMEM((SPAN, D), BF),
            pltpu.VMEM((B, D), BF),
            pltpu.VMEM((B, D), BF),
            pltpu.VMEM((B, D), BF),
            pltpu.VMEM((B, D), BF),
            pltpu.VMEM((VOCAB, B), BF),
            pltpu.VMEM((B, B), F32),
            pltpu.VMEM((REACH + 1, 48, B), F32),
            pltpu.VMEM((2 * B, SPAN), BF),
            pltpu.VMEM((2 * B, SPAN), BF),
            pltpu.VMEM((2, 3, TERM_ROWS, B), BF),
            pltpu.VMEM((3, TERM_ROWS, B), BF),
            pltpu.VMEM((3, TERM_ROWS, B), BF),
            pltpu.VMEM((3, TERM_ROWS, B), BF),
            pltpu.VMEM((TERM_ROWS, B), BF),
            pltpu.VMEM((3, D, B), BF),
            pltpu.VMEM((8, D // 8, B), BF),
            pltpu.VMEM((7, D // 8, B), BF),
            pltpu.VMEM((PAIRS, D // 8, B), BF),
            dma((6,)), dma((8,)), dma((8,)), dma((4,)), dma((4,)), dma((4,)), dma((4,)),
            dma((1,)), dma((1,)), dma((3,)), dma((3,)), dma((3,)), dma((3,)),
            dma((7,)), dma((7,)), dma((7,)), dma((7,)),
        ],
        compiler_params=pltpu.CompilerParams(collective_id=0, has_side_effects=True),
    )(token_ids, cotangent[0], table, w_query, w_key, w_value, w_out, window, *tables)
    return (grad_input[None], weight_grads)


def solution(mesh):
    return jax.shard_map(
        on_device,
        mesh=mesh,
        in_specs=(P("dp", "seq"), P("dp", "seq", None), P(), P(), P(), P(), P(), P()),
        out_specs=(P("dp", "seq", None), P("seq", None)),
        check_vma=False,
    )
```

time: 593 us -> 102 us (0.17)
  waiting for transfers between devices: 421 us -> 0 us
  Pallas kernels: 0 us -> 97.6 us
  matrix products: 63.4 us -> 0 us
  starting transfers between devices: 53.4 us -> 0 us
  local copies, waits for them, and re-layouts: 26.3 us -> 3.31 us
  between operations: 14.8 us -> 0.64 us
  other arithmetic: 11.7 us -> 0 us
    reduce_scatter x1 -> x0, waiting for transfers between devices: 280 us -> none  [on_device(): lax.psum_scatter(term.astype(jnp.bfloat16), 'seq', scatter_dimension=0, t...]
    pallas_call x0 -> x1, Pallas kernels: none -> 97.6 us  [on_device(): pl.pallas_call(kernel, out_shape=(jax.ShapeDtypeStruct((B, D), BF), jax.S...]
    ppermute x16 -> x0, waiting for transfers between devices: 76.3 us -> none  [shifted(): return lax.ppermute(block, axis, route)]
    psum x1 -> x0, waiting for transfers between devices: 65.5 us -> none  [on_device(): weight_grads = lax.psum(shares, 'dp').astype(jnp.float32)]
    dot_general x30 -> x0, matrix products: 63.4 us -> none  [the longest x3 18.1 us: head_group(): jnp.einsum('hqk,qhd->khd', grad_scores, query_heads, preferred_element_ty...]
    ppermute x16 -> x0, starting transfers between devices: 53.3 us -> none  [shifted(): return lax.ppermute(block, axis, route)]
    unnamed x104 -> x2, local copies, waits for them, and re-layouts: 18.4 us -> 3.31 us
  transfers between devices with their start and end apart: 18 -> 0, of which waited for: 7 -> 0; matrix products, arithmetic and copies ran while one was open for 5% -> 0% of each run, Pallas kernels for 0% -> 0%
where the time goes in v1:
time: 102 us
  Pallas kernels  97.6 us (96%)
  local copies, waits for them, and re-layouts  3.31 us (3%)
    pallas_call x1, Pallas kernels, on_device(): pl.pallas_call(kernel, out_shape=(jax.ShapeDtypeStruct((B, D), BF), jax.S...  97.6 us
    unnamed x2, local copies, waits for them, and re-layouts  3.31 us

profile of v1, /device:TPU:1, one launch (start us, length us, event | category | flops | bytes accessed | tf_op | source)
XLA Modules:
  0.0 101.6 jit_solution(17029161619023591905)
XLA Ops:
  0.6 97.6 %shard_map.131 = (bf16[128,768]{1,0:T(8,128)(2,1)}, f32[96,768]{1,0:T(8,128)}) custom-call(s32[1,128]{1,0:T(1,128)} %ids_ref.1, bf16[128,768]{1,0:T(8,128)(2,1)} %bitcast.2, bf16[256,768]{1,0:T(8,128)(2,1)} %table_hbm.1, bf16[768,768]{1,0:T(8,128)(2,1)} %wq_hbm.1, bf16[768,768]{1,0:T(8,128)(2,1)} %wk_hbm.1, bf16[768,768]{1,0:T(8,128)(2,1)} %wv_hbm.1, ...), custom_call_target="tpu_custom_call" | custom-call | tf_op jit(solution)/shard_map/pallas_call | solution.py:452
  98.3 1.6 %copy.16 = bf16[1,128,768]{2,1,0:T(8,128)(2,1)} copy(bf16[1,128,768]{2,1,0:T(8,128)(2,1)} %bitcast.3) | data formatting | bytes 393216
  99.9 1.7 %copy.17 = f32[96,768]{1,0:T(8,128)} copy(f32[96,768]{1,0:T(8,128)} %get-tuple-element.9) | data formatting | bytes 589824

commit v2 on v1

v2 whole, which is shorter than its diff:
```python
import functools

import jax
import jax.numpy as jnp
import numpy as np
from jax import lax
from jax.experimental import pallas as pl
from jax.experimental.pallas import tpu as pltpu
from jax.sharding import PartitionSpec as P

D = 768
HEADS = 12
HEAD_DIM = 64
VOCAB = 256
WINDOW = 512
EPSILON = 1e-05
B = 128
SEQ_DEVS = 32
REACH = WINDOW // B
SPAN = (REACH + 1) * B
PAIRS = D // B
MESH = pl.DeviceIdType.MESH
BF = jnp.bfloat16
F32 = jnp.float32


def rope_tables():
    frequency = 10000.0 ** (-2.0 * np.arange(HEAD_DIM // 2) / HEAD_DIM)
    lane_frequency = np.tile(frequency, 4)[None, :]
    inside = np.arange(B)[:, None] * lane_frequency
    blocks = (np.arange(SEQ_DEVS) * B)[:, None] * lane_frequency
    return [
        np.asarray(part, np.float32)
        for part in (np.cos(inside), np.sin(inside), np.cos(blocks), np.sin(blocks))
    ]


def nn(a, b):
    return lax.dot_general(a, b, (((1,), (0,)), ((), ())), preferred_element_type=F32)


def nt(a, b):
    return lax.dot_general(a, b, (((1,), (1,)), ((), ())), preferred_element_type=F32)


def tn(a, b):
    return lax.dot_general(a, b, (((0,), (0,)), ((), ())), preferred_element_type=F32)


def swap_halves(x):
    lane = lax.broadcasted_iota(jnp.int32, x.shape, 1)
    first = (lane // (HEAD_DIM // 2)) % 2 == 0
    return jnp.where(first, pltpu.roll(x, B - HEAD_DIM // 2, 1), pltpu.roll(x, HEAD_DIM // 2, 1))


def rope(x, cosine, sine):
    return x * cosine + swap_halves(x) * sine


def unrope(x, cosine, sine):
    return x * cosine - swap_halves(x) * sine


def kernel(
    ids_ref, cot_hbm, table_hbm, wq_hbm, wk_hbm, wv_hbm, wo_hbm, window_ref, cr_ref, sr_ref, cb_ref, sb_ref,
    gin_ref, wg_ref,
    ids_all, ids_dp, cot_all, table, wq, wk, wv, wo, ntab, normed, emb, cosv, sinv,
    keys, values, query, gatt, att, gq, gk, gv, statc, stats, probs_s, ds_s, hot_dp,
    q_out, kv_out, q_in, kv_in, tok_sum, tok_in, z_out, z_in, final,
    out_term, out_core, out_x, out_x_in, out_y, out_y_in, out_z, out_z_in, out_final,
    load_sem, ids_send, ids_recv, idp_send, idp_recv, cot_send, cot_recv, st_send, st_recv,
    q_send, q_recv, kv_send, kv_recv, tok_send, tok_recv, z_send, z_recv, fin_send, fin_recv,
    oc_send, oc_recv, ox_send, ox_recv, oy_send, oy_recv, oz_send, oz_recv, of_send,
):
    dp = lax.axis_index("dp")
    sq = lax.axis_index("seq")
    x, z = sq // 8, sq % 8
    y, c = dp // 2, dp % 2
    base = sq * B

    loads = [
        pltpu.make_async_copy(src, dst, load_sem.at[i])
        for i, (src, dst) in enumerate(
            [(cot_hbm, cot_all.at[0]), (table_hbm, table), (wk_hbm, wk), (wv_hbm, wv), (wq_hbm, wq), (wo_hbm, wo)]
        )
    ]
    for load in loads:
        load.start()

    def seq_of(new_x, new_z):
        return new_x * 8 + new_z

    def shift(distance):
        return lax.rem(sq + distance + SEQ_DEVS, SEQ_DEVS)

    def other_dp(step):
        return lax.rem(dp + step, 8)

    def other_y(step):
        return lax.rem(y + step, 4)

    def other_x(step):
        return lax.rem(x + step, 4)

    def other_z(step):
        return lax.rem(z + step, 8)

    barrier = pltpu.get_barrier_semaphore()
    partners = [(dp, shift(d)) for d in (1, 2, 3, 4, -1, -2, -3, -4)]
    partners += [(other_dp(d), sq) for d in range(1, 8)]
    partners += [(dp, seq_of(other_x(d), z)) for d in range(1, 4)]
    partners += [(dp, seq_of(x, other_z(d))) for d in range(1, 8)]
    partners += [(other_dp(e), seq_of(other_x(d), z)) for d in range(1, 4) for e in range(1, 8)]
    for partner in partners:
        pl.semaphore_signal(barrier, inc=1, device_id=partner, device_id_type=MESH)

    lane_row = lax.broadcasted_iota(jnp.int32, (1, B), 1)
    sign = jnp.where((lane_row // (HEAD_DIM // 2)) % 2 == 0, -1.0, 1.0)

    def rope_block(i, carry):
        block = lax.rem(sq + i - REACH + SEQ_DEVS, SEQ_DEVS)
        cb = cb_ref[pl.ds(block, 1), :]
        sb = sb_ref[pl.ds(block, 1), :]
        rows = pl.ds(pl.multiple_of(i * B, B), B)
        cosv[rows, :] = cr_ref[...] * cb - sr_ref[...] * sb
        sinv[rows, :] = (sr_ref[...] * cb + cr_ref[...] * sb) * sign
        return carry

    lax.fori_loop(0, 2 * REACH + 1, rope_block, 0)

    loads[1].wait()
    rows_f = table[...].astype(F32)
    table_inv = lax.rsqrt(jnp.mean(rows_f * rows_f, axis=1, keepdims=True) + EPSILON)
    ntab[...] = (rows_f * table_inv).astype(BF)

    loads[0].wait()
    pl.semaphore_wait(barrier, len(partners))

    def remote(src, dst, send, recv, device):
        return pltpu.make_async_remote_copy(
            src_ref=src, dst_ref=dst, send_sem=send, recv_sem=recv, device_id=device, device_id_type=MESH
        )

    id_copies = []
    for i, d in enumerate((1, 2, 3, 4, -1, -2, -3, -4)):
        id_copies.append(remote(ids_ref, ids_all.at[d + REACH], ids_send.at[i], ids_recv.at[i], (dp, shift(-d))))
    idp_copies = []
    for d in range(1, 8):
        idp_copies.append(
            remote(ids_ref, ids_dp.at[8 - d], idp_send.at[d - 1], idp_recv.at[d - 1], (other_dp(d), sq))
        )
    relays = [
        remote(cot_all.at[step], cot_all.at[step + 1], cot_send.at[step], cot_recv.at[step], (dp, shift(-1)))
        for step in range(REACH)
    ]
    for copy in id_copies:
        copy.start()
    relays[0].start()
    for copy in idp_copies:
        copy.start()
    ids_all[REACH] = ids_ref[...]
    ids_dp[0] = ids_ref[...]

    token = lax.broadcasted_iota(jnp.int32, (VOCAB, B), 0)
    emb[...] = tn((token == ids_ref[...]).astype(BF), table[...])
    loads[5].wait()
    gatt[pl.ds(0, B), :] = nt(cot_all[0], wo[...]).astype(BF)
    for copy in id_copies:
        copy.wait_recv()

    def embed_block(i, carry):
        rows = pl.ds(pl.multiple_of(i * B, B), B)
        hot = (token == ids_all[i]).astype(BF)
        normed[rows, :] = tn(hot, ntab[...]).astype(BF)
        return carry

    lax.fori_loop(0, 2 * REACH + 1, embed_block, 0)

    def project(first, w, out, rotated, scale):
        def slab(j, carry):
            lanes = pl.ds(pl.multiple_of(j * 2 * B, B), 2 * B)
            got = nn(normed[pl.ds(first, SPAN), :], w[:, lanes])
            for half in range(2):
                part = got[:, half * B : (half + 1) * B]
                if rotated:
                    part = rope(part, cosv[pl.ds(first, SPAN), :], sinv[pl.ds(first, SPAN), :])
                out[:, pl.ds(pl.multiple_of((2 * j + half) * B, B), B)] = (
                    (part.astype(BF) * scale).astype(BF) if scale != 1.0 else part.astype(BF)
                )
            return carry

        lax.fori_loop(0, PAIRS // 2, slab, 0)

    loads[2].wait()
    project(0, wk, keys, True, 1.0)
    loads[3].wait()
    project(0, wv, values, False, 1.0)
    relays[0].wait_recv()
    relays[1].start()
    loads[4].wait()
    project(REACH * B, wq, query, True, HEAD_DIM ** (-0.5))

    lane_one = lax.broadcasted_iota(jnp.int32, (1, B), 1)
    left = (lane_one < HEAD_DIM).astype(BF)
    right = (lane_one >= HEAD_DIM).astype(BF)

    def stacked(a):
        return jnp.concatenate([a * left, a * right], axis=0)

    def picked(a):
        return jnp.where(lane_one < HEAD_DIM, a[:B], a[B:])

    own_cos = cosv[pl.ds(REACH * B, B), :]
    own_sin = sinv[pl.ds(REACH * B, B), :]
    statc[...] = jnp.zeros_like(statc)

    def q_copy(p):
        return remote(q_out.at[p], q_in.at[dp], q_send.at[p], q_recv.at[dp], (p, sq))

    def kv_copy(p):
        return remote(kv_out.at[p], kv_in.at[dp], kv_send.at[p], kv_recv.at[dp], (p, sq))

    def pass_one(p, carry):
        lanes = pl.ds(pl.multiple_of(p * B, B), B)
        k, v = keys[:, lanes], values[:, lanes]
        scores = nt(stacked(query[pl.ds(0, B), lanes]), k)
        row = lax.broadcasted_iota(jnp.int32, (2 * B, SPAN), 0)
        col = lax.broadcasted_iota(jnp.int32, (2 * B, SPAN), 1)
        dist = row % B + WINDOW - col
        row_one = lax.broadcasted_iota(jnp.int32, (2 * B, 1), 0)
        width = jnp.where(row_one < B, window_ref[2 * p], window_ref[2 * p + 1])
        allowed = (dist >= 0) & (dist < width) & (col >= WINDOW - base)
        masked = jnp.where(allowed, scores, -1e30)
        top = jnp.max(masked, axis=1, keepdims=True)
        weights = jnp.exp(masked - top)
        scale = 1.0 / jnp.sum(weights, axis=1, keepdims=True)
        probs = weights * scale
        grad_probs = nt(stacked(gatt[pl.ds(0, B), lanes]), v)
        row_term = jnp.sum(probs * grad_probs, axis=1, keepdims=True)
        ds = (probs * (grad_probs - row_term)).astype(BF)
        att[:, lanes] = picked(nn(probs.astype(BF), v)).astype(BF)
        grad_query = picked(nn(ds, k)) * HEAD_DIM ** (-0.5)
        got = unrope(grad_query, own_cos, own_sin).astype(BF)
        gq[:, lanes] = got

        @pl.when(p != dp)
        def _():
            q_out[p] = got
            q_copy(p).start()

        @pl.when(p == dp)
        def _():
            q_in[dp] = got

        held = statc[...]
        for j, stat in enumerate((top, scale, row_term)):
            held = jnp.where(lane_one == 16 * j + 2 * p, stat[:B], held)
            held = jnp.where(lane_one == 16 * j + 2 * p + 1, stat[B:], held)
        statc[...] = held

        @pl.when(p == 2)
        def _():
            relays[1].wait_recv()
            relays[2].start()

        return carry

    lax.fori_loop(0, PAIRS, pass_one, 0)

    stats[0] = statc[...].T[: 3 * 16]
    stat_copies = [
        remote(stats.at[0], stats.at[d], st_send.at[d - 1], st_recv.at[d - 1], (dp, shift(-d)))
        for d in range(1, REACH + 1)
    ]
    for copy in stat_copies:
        copy.start()

    att_t = att[...].T

    def out_terms(p, carry):
        lanes = pl.ds(pl.multiple_of(p * B, B), B)
        got = nn(att_t, cot_all[0, :, lanes]).astype(BF)
        for block in range(4):
            out_term[p % 2, block, p // 2] = got[block * 192 : (block + 1) * 192]
        return carry

    lax.fori_loop(0, PAIRS, out_terms, 0)
    oc = remote(out_term.at[1 - c], out_core, oc_send.at[0], oc_recv.at[0], (y * 2 + 1 - c, sq))
    oc.start()

    for d in range(1, 3):
        gatt[pl.ds(d * B, B), :] = nt(cot_all[d], wo[...]).astype(BF)
    relays[2].wait_recv()
    relays[3].start()
    gatt[pl.ds(3 * B, B), :] = nt(cot_all[3], wo[...]).astype(BF)

    oc.wait_recv()
    for block in range(4):
        out_x[block] = (out_term[c, block].astype(F32) + out_core[block].astype(F32)).astype(BF)

    def ox(step):
        return remote(
            out_x.at[other_x(step)], out_x_in.at[step - 1], ox_send.at[step - 1], ox_recv.at[step - 1],
            (dp, seq_of(other_x(step), z)),
        )

    for step in range(1, 4):
        ox(step).start()

    relays[3].wait_recv()
    gatt[pl.ds(REACH * B, B), :] = nt(cot_all[REACH], wo[...]).astype(BF)
    for copy in stat_copies:
        copy.wait_recv()

    def oy(step):
        return remote(
            out_y.at[lax.min(other_y(step), 2)], out_y_in.at[step - 1], oy_send.at[step - 1], oy_recv.at[step - 1],
            (other_y(step) * 2 + c, sq),
        )

    def pass_two(p, carry):
        lanes = pl.ds(pl.multiple_of(p * B, B), B)
        k2 = stacked(keys[pl.ds(REACH * B, B), lanes])
        v2 = stacked(values[pl.ds(REACH * B, B), lanes])
        row_one = lax.broadcasted_iota(jnp.int32, (2 * B, 1), 0)
        width = jnp.where(row_one < B, window_ref[2 * p], window_ref[2 * p + 1])
        row = lax.broadcasted_iota(jnp.int32, (2 * B, B), 0) % B
        col = lax.broadcasted_iota(jnp.int32, (2 * B, B), 1)
        for d in range(REACH + 1):
            q, g = query[pl.ds(d * B, B), lanes], gatt[pl.ds(d * B, B), lanes]
            dist = col + d * B - row
            allowed = (dist >= 0) & (dist < width) & (col + d * B < SEQ_DEVS * B - base)

            def spread(j):
                a = jnp.broadcast_to(stats[d, pl.ds(16 * j + 2 * p, 1), :], (B, B))
                b = jnp.broadcast_to(stats[d, pl.ds(16 * j + 2 * p + 1, 1), :], (B, B))
                return jnp.concatenate([a, b], axis=0)

            weights = jnp.exp(jnp.where(allowed, nt(k2, q) - spread(0), -1e30))
            probs = weights * spread(1)
            ds = probs * (nt(v2, g) - spread(2))
            probs_s[:, pl.ds(d * B, B)] = probs.astype(BF)
            ds_s[:, pl.ds(d * B, B)] = ds.astype(BF)
        grad_value = picked(nn(probs_s[...], gatt[:, lanes])).astype(BF)
        grad_key = unrope(picked(nn(ds_s[...], query[:, lanes])), own_cos, own_sin).astype(BF)
        gv[:, lanes] = grad_value
        gk[:, lanes] = grad_key

        @pl.when(p != dp)
        def _():
            kv_out[p, 0] = grad_key
            kv_out[p, 1] = grad_value
            kv_copy(p).start()

        @pl.when(p == dp)
        def _():
            kv_in[dp, 0] = grad_key
            kv_in[dp, 1] = grad_value

        @pl.when(p == 4)
        def _():
            for step in range(1, 4):
                ox(step).wait_recv()
            for row in range(3):
                total = out_x[x, row].astype(F32)
                for step in range(3):
                    total += out_x_in[step, row].astype(F32)
                out_y[row] = total.astype(BF)
            for step in range(1, 4):
                @pl.when(other_y(step) < 3)
                def _():
                    oy(step).start()

        return carry

    lax.fori_loop(0, PAIRS, pass_two, 0)

    grad_normed = nt(gq[...], wq[...]) + nt(gk[...], wk[...]) + nt(gv[...], wv[...])
    own = emb[...]
    inv = lax.rsqrt(jnp.mean(own * own, axis=1, keepdims=True) + EPSILON)
    scaled = own * inv
    gin_ref[...] = (
        inv * (grad_normed - scaled * jnp.mean(grad_normed * scaled, axis=1, keepdims=True))
    ).astype(BF)

    def tok(step, target):
        return remote(
            tok_sum.at[target], tok_in.at[step - 1], tok_send.at[step - 1], tok_recv.at[step - 1],
            (dp, seq_of(target, z)),
        )

    def oz_step(i):
        return lax.rem(2 * x + i - z + 8, 8)

    def oz(i):
        step = lax.max(oz_step(i), 1)
        return remote(
            out_z.at[i], out_z_in.at[step - 1], oz_send.at[i], oz_recv.at[step - 1], (dp, seq_of(x, 2 * x + i))
        )

    def oz_in(step):
        return remote(
            out_z.at[0], out_z_in.at[step - 1], oz_send.at[0], oz_recv.at[step - 1], (dp, seq_of(x, z))
        )

    def zs(step):
        return remote(
            z_out.at[other_z(step)], z_in.at[step - 1], z_send.at[step - 1], z_recv.at[step - 1],
            (dp, seq_of(x, other_z(step))),
        )

    mine = lax.min(dp, PAIRS - 1)

    def fin(step):
        return remote(
            final.at[mine], final.at[mine], fin_send.at[step - 1], fin_recv.at[mine], (other_dp(step), sq)
        )

    def out_fin(step):
        return remote(
            out_final, final.at[mine], of_send.at[step], fin_recv.at[mine], (other_dp(step), seq_of(3, z))
        )

    def fin_in(p):
        return remote(final.at[p], final.at[p], fin_send.at[0], fin_recv.at[p], (p, sq))

    for copy in idp_copies:
        copy.wait_recv()

    @pl.when(dp < PAIRS)
    def _():
        def hot_block(i, carry):
            owner = lax.rem(dp + i, 8)
            hot_dp[owner] = (token == ids_dp[i]).astype(BF)
            return carry

        lax.fori_loop(0, 8, hot_block, 0)

        for i in range(8):
            @pl.when(i != dp)
            def _():
                remote(q_out.at[0], q_in.at[i], q_send.at[0], q_recv.at[i], (mine, sq)).wait_recv()

        hot = jnp.concatenate([hot_dp[i] for i in range(8)], axis=1)
        tok_sum[0] = nn(hot, q_in[...].reshape(8 * B, B)).astype(BF)
        for i in range(8):
            @pl.when(i != dp)
            def _():
                remote(kv_out.at[0], kv_in.at[i], kv_send.at[0], kv_recv.at[i], (mine, sq)).wait_recv()
        tok_sum[1] = nn(hot, kv_in[:, 0].reshape(8 * B, B)).astype(BF)
        tok_sum[2] = nn(hot, kv_in[:, 1].reshape(8 * B, B)).astype(BF)
        for step in range(1, 4):
            @pl.when(other_x(step) < 3)
            def _():
                tok(step, lax.min(other_x(step), 2)).start()

        for step in range(1, 4):
            oy(step).wait_recv()
        total = out_y[lax.min(y, 2)].astype(F32)
        for step in range(3):
            total += out_y_in[step].astype(F32)
        out_z[...] = total.astype(BF).reshape(2, D // 8, B)
        for i in range(2):
            @pl.when(oz_step(i) != 0)
            def _():
                oz(i).start()

        @pl.when(x < 3)
        def _():
            for step in range(1, 4):
                tok(step, lax.min(x, 2)).wait_recv()
            total = tok_sum[lax.min(x, 2)].astype(F32)
            for step in range(3):
                total += tok_in[step].astype(F32)
            z_out[...] = tn(ntab[...], total.astype(BF)).astype(BF).reshape(8, D // 8, B)
            for step in range(1, 8):
                zs(step).start()

        @pl.when(z // 2 == x)
        def _():
            for step in range(1, 8):
                oz_in(step).wait_recv()
            total = out_z[z % 2].astype(F32)
            for step in range(7):
                total += out_z_in[step].astype(F32)
            out_final[...] = total.astype(BF)
            for step in range(1, 8):
                out_fin(step).start()

            @pl.when(x < 3)
            def _():
                out_fin(0).start()

            @pl.when(x == 3)
            def _():
                final[mine] = out_final[...]

        @pl.when(x < 3)
        def _():
            for step in range(1, 8):
                zs(step).wait_recv()
            total = z_out[z].astype(F32)
            for step in range(7):
                total += z_in[step].astype(F32)
            final[mine] = total.astype(BF)
            for step in range(1, 8):
                fin(step).start()

    for p in range(PAIRS):
        @pl.when((dp != p) | ((x == 3) & (z < 6)))
        def _():
            fin_in(p).wait_recv()

        wg_ref[:, pl.ds(p * B, B)] = final[p].astype(F32)

    for copy in id_copies + idp_copies + relays + stat_copies + [oc] + [ox(step) for step in range(1, 4)]:
        copy.wait_send()
    for p in range(PAIRS):
        @pl.when(p != dp)
        def _():
            q_copy(p).wait_send()
            kv_copy(p).wait_send()
    for step in range(1, 4):
        @pl.when(other_y(step) < 3)
        def _():
            oy(step).wait_send()

    @pl.when(dp < PAIRS)
    def _():
        for step in range(1, 4):
            @pl.when(other_x(step) < 3)
            def _():
                tok(step, lax.min(other_x(step), 2)).wait_send()
        for i in range(2):
            @pl.when(oz_step(i) != 0)
            def _():
                oz(i).wait_send()

        @pl.when(x < 3)
        def _():
            for step in range(1, 8):
                zs(step).wait_send()
                fin(step).wait_send()

        @pl.when(z // 2 == x)
        def _():
            for step in range(1, 8):
                out_fin(step).wait_send()

            @pl.when(x < 3)
            def _():
                out_fin(0).wait_send()


def on_device(token_ids, cotangent, table, w_query, w_key, w_value, w_out, window):
    tables = [jnp.asarray(part) for part in rope_tables()]
    vmem = pl.BlockSpec(memory_space=pltpu.VMEM)
    hbm = pl.BlockSpec(memory_space=pl.ANY)
    smem = pl.BlockSpec(memory_space=pltpu.SMEM)
    dma = pltpu.SemaphoreType.DMA
    grad_input, weight_grads = pl.pallas_call(
        kernel,
        out_shape=(
            jax.ShapeDtypeStruct((B, D), BF),
            jax.ShapeDtypeStruct((D // 8, D), F32),
        ),
        in_specs=[vmem] + [hbm] * 6 + [smem] + [vmem] * 4,
        out_specs=(vmem, vmem),
        scratch_shapes=[
            pltpu.VMEM((2 * REACH + 1, 1, B), jnp.int32),
            pltpu.VMEM((8, 1, B), jnp.int32),
            pltpu.VMEM((REACH + 1, B, D), BF),
            pltpu.VMEM((VOCAB, D), BF),
            pltpu.VMEM((D, D), BF),
            pltpu.VMEM((D, D), BF),
            pltpu.VMEM((D, D), BF),
            pltpu.VMEM((D, D), BF),
            pltpu.VMEM((VOCAB, D), BF),
            pltpu.VMEM(((2 * REACH + 1) * B, D), BF),
            pltpu.VMEM((B, D), F32),
            pltpu.VMEM(((2 * REACH + 1) * B, B), F32),
            pltpu.VMEM(((2 * REACH + 1) * B, B), F32),
            pltpu.VMEM((SPAN, D), BF),
            pltpu.VMEM((SPAN, D), BF),
            pltpu.VMEM((SPAN, D), BF),
            pltpu.VMEM((SPAN, D), BF),
            pltpu.VMEM((B, D), BF),
            pltpu.VMEM((B, D), BF),
            pltpu.VMEM((B, D), BF),
            pltpu.VMEM((B, D), BF),
            pltpu.VMEM((B, B), F32),
            pltpu.VMEM((REACH + 1, 48, B), F32),
            pltpu.VMEM((2 * B, SPAN), BF),
            pltpu.VMEM((2 * B, SPAN), BF),
            pltpu.VMEM((8, VOCAB, B), BF),
            pltpu.VMEM((PAIRS, B, B), BF),
            pltpu.VMEM((PAIRS, 2, B, B), BF),
            pltpu.VMEM((8, B, B), BF),
            pltpu.VMEM((8, 2, B, B), BF),
            pltpu.VMEM((3, VOCAB, B), BF),
            pltpu.VMEM((3, VOCAB, B), BF),
            pltpu.VMEM((8, D // 8, B), BF),
            pltpu.VMEM((7, D // 8, B), BF),
            pltpu.VMEM((PAIRS, D // 8, B), BF),
            pltpu.VMEM((2, 4, 3, D // 4, B), BF),
            pltpu.VMEM((4, 3, D // 4, B), BF),
            pltpu.VMEM((4, 3, D // 4, B), BF),
            pltpu.VMEM((3, 3, D // 4, B), BF),
            pltpu.VMEM((3, D // 4, B), BF),
            pltpu.VMEM((3, D // 4, B), BF),
            pltpu.VMEM((2, D // 8, B), BF),
            pltpu.VMEM((7, D // 8, B), BF),
            pltpu.VMEM((D // 8, B), BF),
            dma((6,)), dma((8,)), dma((8,)), dma((7,)), dma((7,)), dma((4,)), dma((4,)), dma((4,)), dma((4,)),
            dma((PAIRS,)), dma((8,)), dma((PAIRS,)), dma((8,)), dma((3,)), dma((3,)), dma((7,)), dma((7,)),
            dma((7,)), dma((PAIRS,)),
            dma((1,)), dma((1,)), dma((3,)), dma((3,)), dma((3,)), dma((3,)), dma((2,)), dma((7,)), dma((8,)),
        ],
        compiler_params=pltpu.CompilerParams(collective_id=0, has_side_effects=True),
    )(token_ids, cotangent[0], table, w_query, w_key, w_value, w_out, window, *tables)
    return (grad_input[None], weight_grads)


def solution(mesh):
    return jax.shard_map(
        on_device,
        mesh=mesh,
        in_specs=(P("dp", "seq"), P("dp", "seq", None), P(), P(), P(), P(), P(), P()),
        out_specs=(P("dp", "seq", None), P("seq", None)),
        check_vma=False,
    )
```

time: 102 us -> 76.1 us (0.75)
  Pallas kernels: 97.6 us -> 71.9 us
    pallas_call x1, Pallas kernels: 97.6 us -> 71.9 us  [on_device(): pl.pallas_call(kernel, out_shape=(jax.ShapeDtypeStruct((B, D), BF), jax.S...]
where the time goes in v2:
time: 76.1 us; the launch traced here: 75.9 us
  Pallas kernels  71.9 us (94%)
  local copies, waits for them, and re-layouts  3.31 us (4%)
    pallas_call x1, Pallas kernels, on_device(): pl.pallas_call(kernel, out_shape=(jax.ShapeDtypeStruct((B, D), BF), jax.S...  71.9 us
    unnamed x2, local copies, waits for them, and re-layouts  3.31 us

profile of v2, /device:TPU:1, one launch (start us, length us, event | category | flops | bytes accessed | tf_op | source)
XLA Modules:
  0.0 75.9 jit_solution(11301336466230611509)
XLA Ops:
  0.6 71.9 %shard_map.131 = (bf16[128,768]{1,0:T(8,128)(2,1)}, f32[96,768]{1,0:T(8,128)}) custom-call(s32[1,128]{1,0:T(1,128)} %ids_ref.1, bf16[128,768]{1,0:T(8,128)(2,1)} %bitcast.2, bf16[256,768]{1,0:T(8,128)(2,1)} %table_hbm.1, bf16[768,768]{1,0:T(8,128)(2,1)} %wq_hbm.1, bf16[768,768]{1,0:T(8,128)(2,1)} %wk_hbm.1, bf16[768,768]{1,0:T(8,128)(2,1)} %wv_hbm.1, ...), custom_call_target="tpu_custom_call" | custom-call | tf_op jit(solution)/shard_map/pallas_call | solution.py:561
  72.6 1.6 %copy.16 = bf16[1,128,768]{2,1,0:T(8,128)(2,1)} copy(bf16[1,128,768]{2,1,0:T(8,128)(2,1)} %bitcast.3) | data formatting | bytes 393216
  74.2 1.7 %copy.17 = f32[96,768]{1,0:T(8,128)} copy(f32[96,768]{1,0:T(8,128)} %get-tuple-element.9) | data formatting | bytes 589824

commit v3 on v2

--- a/solution.py
+++ b/solution.py
@@ -64,13 +64,13 @@
 def kernel(
     ids_ref, cot_hbm, table_hbm, wq_hbm, wk_hbm, wv_hbm, wo_hbm, window_ref, cr_ref, sr_ref, cb_ref, sb_ref,
     gin_ref, wg_ref,
-    ids_all, ids_dp, cot_all, table, wq, wk, wv, wo, ntab, normed, emb, cosv, sinv,
+    ids_all, ids_dp, cot_all, table, wq, wk, wv, wo, ntab, qtab, ktab, vtab, hot, emb, cosv, sinv, seen, seeing,
     keys, values, query, gatt, att, gq, gk, gv, statc, stats, probs_s, ds_s, hot_dp,
     q_out, kv_out, q_in, kv_in, tok_sum, tok_in, z_out, z_in, final,
     out_term, out_core, out_x, out_x_in, out_y, out_y_in, out_z, out_z_in, out_final,
     load_sem, ids_send, ids_recv, idp_send, idp_recv, cot_send, cot_recv, st_send, st_recv,
     q_send, q_recv, kv_send, kv_recv, tok_send, tok_recv, z_send, z_recv, fin_send, fin_recv,
-    oc_send, oc_recv, ox_send, ox_recv, oy_send, oy_recv, oz_send, oz_recv, of_send,
+    oc_send, oc_recv, ox_send, ox_recv, oy_send, oy_recv, oz_send, oz_recv, of_send, of_recv,
 ):
     dp = lax.axis_index("dp")
     sq = lax.axis_index("seq")
@@ -81,7 +81,7 @@
     loads = [
         pltpu.make_async_copy(src, dst, load_sem.at[i])
         for i, (src, dst) in enumerate(
-            [(cot_hbm, cot_all.at[0]), (table_hbm, table), (wk_hbm, wk), (wv_hbm, wv), (wq_hbm, wq), (wo_hbm, wo)]
+            [(table_hbm, table), (cot_hbm, cot_all.at[0]), (wk_hbm, wk), (wv_hbm, wv), (wq_hbm, wq), (wo_hbm, wo)]
         )
     ]
     for load in loads:
@@ -110,7 +110,6 @@
     partners += [(other_dp(d), sq) for d in range(1, 8)]
     partners += [(dp, seq_of(other_x(d), z)) for d in range(1, 4)]
     partners += [(dp, seq_of(x, other_z(d))) for d in range(1, 8)]
-    partners += [(other_dp(e), seq_of(other_x(d), z)) for d in range(1, 4) for e in range(1, 8)]
     for partner in partners:
         pl.semaphore_signal(barrier, inc=1, device_id=partner, device_id_type=MESH)
 
@@ -128,12 +127,22 @@
 
     lax.fori_loop(0, 2 * REACH + 1, rope_block, 0)
 
-    loads[1].wait()
+    loads[0].wait()
     rows_f = table[...].astype(F32)
     table_inv = lax.rsqrt(jnp.mean(rows_f * rows_f, axis=1, keepdims=True) + EPSILON)
     ntab[...] = (rows_f * table_inv).astype(BF)
 
-    loads[0].wait()
+    def project_table(w, out):
+        def slab(j, carry):
+            lanes = pl.ds(pl.multiple_of(j * 2 * B, B), 2 * B)
+            out[:, lanes] = nn(ntab[...], w[:, lanes]).astype(BF)
+            return carry
+
+        lax.fori_loop(0, PAIRS // 2, slab, 0)
+
+    loads[2].wait()
+    project_table(wk, ktab)
+    loads[1].wait()
     pl.semaphore_wait(barrier, len(partners))
 
     def remote(src, dst, send, recv, device):
@@ -161,44 +170,51 @@
     ids_all[REACH] = ids_ref[...]
     ids_dp[0] = ids_ref[...]
 
-    token = lax.broadcasted_iota(jnp.int32, (VOCAB, B), 0)
-    emb[...] = tn((token == ids_ref[...]).astype(BF), table[...])
+    loads[3].wait()
+    project_table(wv, vtab)
+    loads[4].wait()
+    project_table(wq, qtab)
     loads[5].wait()
     gatt[pl.ds(0, B), :] = nt(cot_all[0], wo[...]).astype(BF)
+
+    far = 1 << 20
+    dist = lax.broadcasted_iota(jnp.int32, (B, SPAN), 0) + WINDOW - lax.broadcasted_iota(jnp.int32, (B, SPAN), 1)
+    col = lax.broadcasted_iota(jnp.int32, (B, SPAN), 1)
+    seen[...] = jnp.where((dist >= 0) & (col >= WINDOW - base), dist, far)
+    dist = col - lax.broadcasted_iota(jnp.int32, (B, SPAN), 0)
+    seeing[...] = jnp.where((dist >= 0) & (col < SEQ_DEVS * B - base), dist, far)
+
     for copy in id_copies:
         copy.wait_recv()
 
-    def embed_block(i, carry):
-        rows = pl.ds(pl.multiple_of(i * B, B), B)
-        hot = (token == ids_all[i]).astype(BF)
-        normed[rows, :] = tn(hot, ntab[...]).astype(BF)
+    token = lax.broadcasted_iota(jnp.int32, (VOCAB, B), 0)
+
+    def hot_rows(i, carry):
+        hot[pl.ds(pl.multiple_of(i * B, B), B), :] = (token == ids_all[i]).astype(F32).T.astype(BF)
         return carry
 
-    lax.fori_loop(0, 2 * REACH + 1, embed_block, 0)
-
-    def project(first, w, out, rotated, scale):
+    lax.fori_loop(0, 2 * REACH + 1, hot_rows, 0)
+
+    def select(tab, out, first, to, count, rotated, scale):
         def slab(j, carry):
             lanes = pl.ds(pl.multiple_of(j * 2 * B, B), 2 * B)
-            got = nn(normed[pl.ds(first, SPAN), :], w[:, lanes])
+            got = nn(hot[pl.ds(first, count), :], tab[:, lanes])
             for half in range(2):
                 part = got[:, half * B : (half + 1) * B]
                 if rotated:
-                    part = rope(part, cosv[pl.ds(first, SPAN), :], sinv[pl.ds(first, SPAN), :])
-                out[:, pl.ds(pl.multiple_of((2 * j + half) * B, B), B)] = (
-                    (part.astype(BF) * scale).astype(BF) if scale != 1.0 else part.astype(BF)
-                )
+                    part = rope(part, cosv[pl.ds(first, count), :], sinv[pl.ds(first, count), :])
+                if scale != 1.0:
+                    part = part * scale
+                out[pl.ds(to, count), pl.ds(pl.multiple_of((2 * j + half) * B, B), B)] = part.astype(BF)
             return carry
 
         lax.fori_loop(0, PAIRS // 2, slab, 0)
 
-    loads[2].wait()
-    project(0, wk, keys, True, 1.0)
-    loads[3].wait()
-    project(0, wv, values, False, 1.0)
+    select(ktab, keys, 0, 0, SPAN, True, 1.0)
     relays[0].wait_recv()
     relays[1].start()
-    loads[4].wait()
-    project(REACH * B, wq, query, True, HEAD_DIM ** (-0.5))
+    select(vtab, values, 0, 0, SPAN, False, 1.0)
+    select(qtab, query, REACH * B, 0, B, True, HEAD_DIM ** (-0.5))
 
     lane_one = lax.broadcasted_iota(jnp.int32, (1, B), 1)
     left = (lane_one < HEAD_DIM).astype(BF)
@@ -224,17 +240,18 @@
         lanes = pl.ds(pl.multiple_of(p * B, B), B)
         k, v = keys[:, lanes], values[:, lanes]
         scores = nt(stacked(query[pl.ds(0, B), lanes]), k)
-        row = lax.broadcasted_iota(jnp.int32, (2 * B, SPAN), 0)
-        col = lax.broadcasted_iota(jnp.int32, (2 * B, SPAN), 1)
-        dist = row % B + WINDOW - col
-        row_one = lax.broadcasted_iota(jnp.int32, (2 * B, 1), 0)
-        width = jnp.where(row_one < B, window_ref[2 * p], window_ref[2 * p + 1])
-        allowed = (dist >= 0) & (dist < width) & (col >= WINDOW - base)
-        masked = jnp.where(allowed, scores, -1e30)
+        reach = seen[...]
+        masked = jnp.concatenate(
+            [
+                jnp.where(reach < window_ref[2 * p], scores[:B], -1e30),
+                jnp.where(reach < window_ref[2 * p + 1], scores[B:], -1e30),
+            ],
+            axis=0,
+        )
         top = jnp.max(masked, axis=1, keepdims=True)
         weights = jnp.exp(masked - top)
-        scale = 1.0 / jnp.sum(weights, axis=1, keepdims=True)
-        probs = weights * scale
+        whole = jnp.sum(weights, axis=1, keepdims=True)
+        probs = weights * (1.0 / whole)
         grad_probs = nt(stacked(gatt[pl.ds(0, B), lanes]), v)
         row_term = jnp.sum(probs * grad_probs, axis=1, keepdims=True)
         ds = (probs * (grad_probs - row_term)).astype(BF)
@@ -253,12 +270,12 @@
             q_in[dp] = got
 
         held = statc[...]
-        for j, stat in enumerate((top, scale, row_term)):
+        for j, stat in enumerate((top + jnp.log(whole), row_term)):
             held = jnp.where(lane_one == 16 * j + 2 * p, stat[:B], held)
             held = jnp.where(lane_one == 16 * j + 2 * p + 1, stat[B:], held)
         statc[...] = held
 
-        @pl.when(p == 2)
+        @pl.when(p == 5)
         def _():
             relays[1].wait_recv()
             relays[2].start()
@@ -267,7 +284,7 @@
 
     lax.fori_loop(0, PAIRS, pass_one, 0)
 
-    stats[0] = statc[...].T[: 3 * 16]
+    stats[0] = statc[...].T[: 2 * 16]
     stat_copies = [
         remote(stats.at[0], stats.at[d], st_send.at[d - 1], st_recv.at[d - 1], (dp, shift(-d)))
         for d in range(1, REACH + 1)
@@ -275,6 +292,9 @@
     for copy in stat_copies:
         copy.start()
 
+    emb[...] = nn(hot[pl.ds(REACH * B, B), :], table[...])
+    select(qtab, query, (REACH + 1) * B, B, REACH * B, True, HEAD_DIM ** (-0.5))
+
     att_t = att[...].T
 
     def out_terms(p, carry):
@@ -322,23 +342,18 @@
         lanes = pl.ds(pl.multiple_of(p * B, B), B)
         k2 = stacked(keys[pl.ds(REACH * B, B), lanes])
         v2 = stacked(values[pl.ds(REACH * B, B), lanes])
-        row_one = lax.broadcasted_iota(jnp.int32, (2 * B, 1), 0)
-        width = jnp.where(row_one < B, window_ref[2 * p], window_ref[2 * p + 1])
-        row = lax.broadcasted_iota(jnp.int32, (2 * B, B), 0) % B
-        col = lax.broadcasted_iota(jnp.int32, (2 * B, B), 1)
         for d in range(REACH + 1):
             q, g = query[pl.ds(d * B, B), lanes], gatt[pl.ds(d * B, B), lanes]
-            dist = col + d * B - row
-            allowed = (dist >= 0) & (dist < width) & (col + d * B < SEQ_DEVS * B - base)
+            reach = seeing[:, pl.ds(d * B, B)]
+            allowed = jnp.concatenate([reach < window_ref[2 * p], reach < window_ref[2 * p + 1]], axis=0)
 
             def spread(j):
                 a = jnp.broadcast_to(stats[d, pl.ds(16 * j + 2 * p, 1), :], (B, B))
                 b = jnp.broadcast_to(stats[d, pl.ds(16 * j + 2 * p + 1, 1), :], (B, B))
                 return jnp.concatenate([a, b], axis=0)
 
-            weights = jnp.exp(jnp.where(allowed, nt(k2, q) - spread(0), -1e30))
-            probs = weights * spread(1)
-            ds = probs * (nt(v2, g) - spread(2))
+            probs = jnp.exp(jnp.where(allowed, nt(k2, q) - spread(0), -1e30))
+            ds = probs * (nt(v2, g) - spread(1))
             probs_s[:, pl.ds(d * B, B)] = probs.astype(BF)
             ds_s[:, pl.ds(d * B, B)] = ds.astype(BF)
         grad_value = picked(nn(probs_s[...], gatt[:, lanes])).astype(BF)
@@ -416,10 +431,8 @@
             final.at[mine], final.at[mine], fin_send.at[step - 1], fin_recv.at[mine], (other_dp(step), sq)
         )
 
-    def out_fin(step):
-        return remote(
-            out_final, final.at[mine], of_send.at[step], fin_recv.at[mine], (other_dp(step), seq_of(3, z))
-        )
+    def out_fin():
+        return remote(out_final, final.at[mine], of_send.at[0], of_recv.at[0], (dp, seq_of(3, z)))
 
     def fin_in(p):
         return remote(final.at[p], final.at[p], fin_send.at[0], fin_recv.at[p], (p, sq))
@@ -484,12 +497,10 @@
             for step in range(7):
                 total += out_z_in[step].astype(F32)
             out_final[...] = total.astype(BF)
-            for step in range(1, 8):
-                out_fin(step).start()
 
             @pl.when(x < 3)
             def _():
-                out_fin(0).start()
+                out_fin().start()
 
             @pl.when(x == 3)
             def _():
@@ -503,11 +514,16 @@
             for step in range(7):
                 total += z_in[step].astype(F32)
             final[mine] = total.astype(BF)
-            for step in range(1, 8):
-                fin(step).start()
+
+        @pl.when((x == 3) & (z < 6))
+        def _():
+            out_fin().wait_recv()
+
+        for step in range(1, 8):
+            fin(step).start()
 
     for p in range(PAIRS):
-        @pl.when((dp != p) | ((x == 3) & (z < 6)))
+        @pl.when(dp != p)
         def _():
             fin_in(p).wait_recv()
 
@@ -540,16 +556,13 @@
         def _():
             for step in range(1, 8):
                 zs(step).wait_send()
-                fin(step).wait_send()
-
-        @pl.when(z // 2 == x)
-        def _():
-            for step in range(1, 8):
-                out_fin(step).wait_send()
-
-            @pl.when(x < 3)
-            def _():
-                out_fin(0).wait_send()
+
+        @pl.when((z // 2 == x) & (x < 3))
+        def _():
+            out_fin().wait_send()
+
+        for step in range(1, 8):
+            fin(step).wait_send()
 
 
 def on_device(token_ids, cotangent, table, w_query, w_key, w_value, w_out, window):
@@ -576,10 +589,15 @@
             pltpu.VMEM((D, D), BF),
             pltpu.VMEM((D, D), BF),
             pltpu.VMEM((VOCAB, D), BF),
-            pltpu.VMEM(((2 * REACH + 1) * B, D), BF),
+            pltpu.VMEM((VOCAB, D), BF),
+            pltpu.VMEM((VOCAB, D), BF),
+            pltpu.VMEM((VOCAB, D), BF),
+            pltpu.VMEM(((2 * REACH + 1) * B, VOCAB), BF),
             pltpu.VMEM((B, D), F32),
             pltpu.VMEM(((2 * REACH + 1) * B, B), F32),
             pltpu.VMEM(((2 * REACH + 1) * B, B), F32),
+            pltpu.VMEM((B, SPAN), jnp.int32),
+            pltpu.VMEM((B, SPAN), jnp.int32),
             pltpu.VMEM((SPAN, D), BF),
             pltpu.VMEM((SPAN, D), BF),
             pltpu.VMEM((SPAN, D), BF),
@@ -589,7 +607,7 @@
             pltpu.VMEM((B, D), BF),
             pltpu.VMEM((B, D), BF),
             pltpu.VMEM((B, B), F32),
-            pltpu.VMEM((REACH + 1, 48, B), F32),
+            pltpu.VMEM((REACH + 1, 32, B), F32),
             pltpu.VMEM((2 * B, SPAN), BF),
             pltpu.VMEM((2 * B, SPAN), BF),
             pltpu.VMEM((8, VOCAB, B), BF),
@@ -614,7 +632,7 @@
             dma((6,)), dma((8,)), dma((8,)), dma((7,)), dma((7,)), dma((4,)), dma((4,)), dma((4,)), dma((4,)),
             dma((PAIRS,)), dma((8,)), dma((PAIRS,)), dma((8,)), dma((3,)), dma((3,)), dma((7,)), dma((7,)),
             dma((7,)), dma((PAIRS,)),
-            dma((1,)), dma((1,)), dma((3,)), dma((3,)), dma((3,)), dma((3,)), dma((2,)), dma((7,)), dma((8,)),
+            dma((1,)), dma((1,)), dma((3,)), dma((3,)), dma((3,)), dma((3,)), dma((2,)), dma((7,)), dma((1,)), dma((1,)),
         ],
         compiler_params=pltpu.CompilerParams(collective_id=0, has_side_effects=True),
     )(token_ids, cotangent[0], table, w_query, w_key, w_value, w_out, window, *tables)

time: 76.1 us -> 74 us (0.972)
  Pallas kernels: 71.9 us -> 69.9 us
    pallas_call x1, Pallas kernels: 71.9 us -> 69.9 us  [on_device(): pl.pallas_call(kernel, out_shape=(jax.ShapeDtypeStruct((B, D), BF), jax.S...]
where the time goes in v3:
time: 74 us; the launch traced here: 73.8 us
  Pallas kernels  69.9 us (94%)
  local copies, waits for them, and re-layouts  3.31 us (4%)
    pallas_call x1, Pallas kernels, on_device(): pl.pallas_call(kernel, out_shape=(jax.ShapeDtypeStruct((B, D), BF), jax.S...  69.9 us
    unnamed x2, local copies, waits for them, and re-layouts  3.31 us

profile of v3, /device:TPU:1, one launch (start us, length us, event | category | flops | bytes accessed | tf_op | source)
XLA Modules:
  0.0 73.8 jit_solution(5627204959356139934)
XLA Ops:
  0.6 69.9 %shard_map.131 = (bf16[128,768]{1,0:T(8,128)(2,1)}, f32[96,768]{1,0:T(8,128)}) custom-call(s32[1,128]{1,0:T(1,128)} %ids_ref.1, bf16[128,768]{1,0:T(8,128)(2,1)} %bitcast.2, bf16[256,768]{1,0:T(8,128)(2,1)} %table_hbm.1, bf16[768,768]{1,0:T(8,128)(2,1)} %wq_hbm.1, bf16[768,768]{1,0:T(8,128)(2,1)} %wk_hbm.1, bf16[768,768]{1,0:T(8,128)(2,1)} %wv_hbm.1, ...), custom_call_target="tpu_custom_call" | custom-call | tf_op jit(solution)/shard_map/pallas_call | solution.py:574
  70.5 1.6 %copy.16 = bf16[1,128,768]{2,1,0:T(8,128)(2,1)} copy(bf16[1,128,768]{2,1,0:T(8,128)(2,1)} %bitcast.3) | data formatting | bytes 393216
  72.1 1.7 %copy.17 = f32[96,768]{1,0:T(8,128)} copy(f32[96,768]{1,0:T(8,128)} %get-tuple-element.9) | data formatting | bytes 589824

commit v4 on v3

--- a/solution.py
+++ b/solution.py
@@ -63,10 +63,10 @@
 
 def kernel(
     ids_ref, cot_hbm, table_hbm, wq_hbm, wk_hbm, wv_hbm, wo_hbm, window_ref, cr_ref, sr_ref, cb_ref, sb_ref,
-    gin_ref, wg_ref,
-    ids_all, ids_dp, cot_all, table, wq, wk, wv, wo, ntab, qtab, ktab, vtab, hot, emb, cosv, sinv, seen, seeing,
+    gin_ref, final,
+    ids_all, ids_dp, cot_all, table, wq, wk, wv, wo, ntab_t, ntab, qtab, ktab, vtab, hot, emb, cosv, sinv, seen, seeing,
     keys, values, query, gatt, att, gq, gk, gv, statc, stats, probs_s, ds_s, hot_dp,
-    q_out, kv_out, q_in, kv_in, tok_sum, tok_in, z_out, z_in, final,
+    q_out, kv_out, q_in, kv_in, tok_sum, tok_in, z_out, z_in,
     out_term, out_core, out_x, out_x_in, out_y, out_y_in, out_z, out_z_in, out_final,
     load_sem, ids_send, ids_recv, idp_send, idp_recv, cot_send, cot_recv, st_send, st_recv,
     q_send, q_recv, kv_send, kv_recv, tok_send, tok_recv, z_send, z_recv, fin_send, fin_recv,
@@ -113,6 +113,43 @@
     for partner in partners:
         pl.semaphore_signal(barrier, inc=1, device_id=partner, device_id_type=MESH)
 
+    pl.semaphore_wait(barrier, len(partners))
+
+    def remote(src, dst, send, recv, device):
+        return pltpu.make_async_remote_copy(
+            src_ref=src, dst_ref=dst, send_sem=send, recv_sem=recv, device_id=device, device_id_type=MESH
+        )
+
+    id_copies = []
+    for i, d in enumerate((4, -4, 3, -3, 2, -2, 1, -1)):
+        id_copies.append(remote(ids_ref, ids_all.at[d + REACH], ids_send.at[i], ids_recv.at[i], (dp, shift(-d))))
+    idp_copies = []
+    for d in range(1, 8):
+        idp_copies.append(
+            remote(ids_ref, ids_dp.at[8 - d], idp_send.at[d - 1], idp_recv.at[d - 1], (other_dp(d), sq))
+        )
+
+    def relay(step, half):
+        rows = pl.ds(half * (B // 2), B // 2)
+        source = cot_hbm.at[rows] if step == 0 else cot_all.at[step, rows]
+        return remote(
+            source, cot_all.at[step + 1, rows], cot_send.at[2 * step + half], cot_recv.at[2 * step + half],
+            (dp, shift(-1)),
+        )
+
+    def forward(step, half):
+        relay(step - 1, half).wait_recv()
+        relay(step, half).start()
+
+    for copy in id_copies:
+        copy.start()
+    relay(0, 0).start()
+    relay(0, 1).start()
+    for copy in idp_copies:
+        copy.start()
+    ids_all[REACH] = ids_ref[...]
+    ids_dp[0] = ids_ref[...]
+
     lane_row = lax.broadcasted_iota(jnp.int32, (1, B), 1)
     sign = jnp.where((lane_row // (HEAD_DIM // 2)) % 2 == 0, -1.0, 1.0)
 
@@ -142,39 +179,13 @@
 
     loads[2].wait()
     project_table(wk, ktab)
-    loads[1].wait()
-    pl.semaphore_wait(barrier, len(partners))
-
-    def remote(src, dst, send, recv, device):
-        return pltpu.make_async_remote_copy(
-            src_ref=src, dst_ref=dst, send_sem=send, recv_sem=recv, device_id=device, device_id_type=MESH
-        )
-
-    id_copies = []
-    for i, d in enumerate((1, 2, 3, 4, -1, -2, -3, -4)):
-        id_copies.append(remote(ids_ref, ids_all.at[d + REACH], ids_send.at[i], ids_recv.at[i], (dp, shift(-d))))
-    idp_copies = []
-    for d in range(1, 8):
-        idp_copies.append(
-            remote(ids_ref, ids_dp.at[8 - d], idp_send.at[d - 1], idp_recv.at[d - 1], (other_dp(d), sq))
-        )
-    relays = [
-        remote(cot_all.at[step], cot_all.at[step + 1], cot_send.at[step], cot_recv.at[step], (dp, shift(-1)))
-        for step in range(REACH)
-    ]
-    for copy in id_copies:
-        copy.start()
-    relays[0].start()
-    for copy in idp_copies:
-        copy.start()
-    ids_all[REACH] = ids_ref[...]
-    ids_dp[0] = ids_ref[...]
-
     loads[3].wait()
     project_table(wv, vtab)
+    forward(1, 0)
     loads[4].wait()
     project_table(wq, qtab)
     loads[5].wait()
+    loads[1].wait()
     gatt[pl.ds(0, B), :] = nt(cot_all[0], wo[...]).astype(BF)
 
     far = 1 << 20
@@ -210,11 +221,11 @@
 
         lax.fori_loop(0, PAIRS // 2, slab, 0)
 
+    forward(1, 1)
     select(ktab, keys, 0, 0, SPAN, True, 1.0)
-    relays[0].wait_recv()
-    relays[1].start()
     select(vtab, values, 0, 0, SPAN, False, 1.0)
     select(qtab, query, REACH * B, 0, B, True, HEAD_DIM ** (-0.5))
+    forward(2, 0)
 
     lane_one = lax.broadcasted_iota(jnp.int32, (1, B), 1)
     left = (lane_one < HEAD_DIM).astype(BF)
@@ -235,6 +246,10 @@
 
     def kv_copy(p):
         return remote(kv_out.at[p], kv_in.at[dp], kv_send.at[p], kv_recv.at[dp], (p, sq))
+
+    def stat_copy(part, d):
+        at = REACH * part + d - 1
+        return remote(stats.at[part, 0], stats.at[part, d], st_send.at[at], st_recv.at[at], (dp, shift(-d)))
 
     def pass_one(p, carry):
         lanes = pl.ds(pl.multiple_of(p * B, B), B)
@@ -271,27 +286,35 @@
 
         held = statc[...]
         for j, stat in enumerate((top + jnp.log(whole), row_term)):
-            held = jnp.where(lane_one == 16 * j + 2 * p, stat[:B], held)
-            held = jnp.where(lane_one == 16 * j + 2 * p + 1, stat[B:], held)
+            first = 16 * (p // 3) + 8 * j + 2 * (p % 3)
+            held = jnp.where(lane_one == first, stat[:B], held)
+            held = jnp.where(lane_one == first + 1, stat[B:], held)
         statc[...] = held
 
-        @pl.when(p == 5)
-        def _():
-            relays[1].wait_recv()
-            relays[2].start()
+        @pl.when(p == 1)
+        def _():
+            forward(2, 1)
+
+        @pl.when(p == 2)
+        def _():
+            stats[0, 0] = statc[...].T[:16]
+            for d in range(REACH, 0, -1):
+                stat_copy(0, d).start()
+
+        @pl.when(p == 3)
+        def _():
+            forward(3, 0)
 
         return carry
 
     lax.fori_loop(0, PAIRS, pass_one, 0)
 
-    stats[0] = statc[...].T[: 2 * 16]
-    stat_copies = [
-        remote(stats.at[0], stats.at[d], st_send.at[d - 1], st_recv.at[d - 1], (dp, shift(-d)))
-        for d in range(1, REACH + 1)
-    ]
-    for copy in stat_copies:
-        copy.start()
-
+    stats[1, 0] = statc[...].T[16:32]
+    for d in range(REACH, 0, -1):
+        stat_copy(1, d).start()
+    forward(3, 1)
+
+    ntab_t[...] = ntab[...].T
     emb[...] = nn(hot[pl.ds(REACH * B, B), :], table[...])
     select(qtab, query, (REACH + 1) * B, B, REACH * B, True, HEAD_DIM ** (-0.5))
 
@@ -308,11 +331,47 @@
     oc = remote(out_term.at[1 - c], out_core, oc_send.at[0], oc_recv.at[0], (y * 2 + 1 - c, sq))
     oc.start()
 
-    for d in range(1, 3):
+    for d in range(1, 4):
         gatt[pl.ds(d * B, B), :] = nt(cot_all[d], wo[...]).astype(BF)
-    relays[2].wait_recv()
-    relays[3].start()
-    gatt[pl.ds(3 * B, B), :] = nt(cot_all[3], wo[...]).astype(BF)
+
+    def tok(step, target):
+        return remote(
+            tok_sum.at[target], tok_in.at[step - 1], tok_send.at[step - 1], tok_recv.at[step - 1],
+            (dp, seq_of(target, z)),
+        )
+
+    def oz_step(i):
+        return lax.rem(2 * x + i - z + 8, 8)
+
+    def oz(i):
+        step = lax.max(oz_step(i), 1)
+        return remote(
+            out_z.at[i], out_z_in.at[step - 1], oz_send.at[i], oz_recv.at[step - 1], (dp, seq_of(x, 2 * x + i))
+        )
+
+    def oz_in(step):
+        return remote(
+            out_z.at[0], out_z_in.at[step - 1], oz_send.at[0], oz_recv.at[step - 1], (dp, seq_of(x, z))
+        )
+
+    def zs(step):
+        return remote(
+            z_out.at[other_z(step)], z_in.at[step - 1], z_send.at[step - 1], z_recv.at[step - 1],
+            (dp, seq_of(x, other_z(step))),
+        )
+
+    mine = lax.min(dp, PAIRS - 1)
+
+    def fin(step):
+        return remote(
+            final.at[mine], final.at[mine], fin_send.at[step - 1], fin_recv.at[mine], (other_dp(step), sq)
+        )
+
+    def out_fin():
+        return remote(out_final, final.at[mine], of_send.at[0], of_recv.at[0], (dp, seq_of(3, z)))
+
+    def fin_in(p):
+        return remote(final.at[p], final.at[p], fin_send.at[0], fin_recv.at[p], (p, sq))
 
     oc.wait_recv()
     for block in range(4):
@@ -327,10 +386,37 @@
     for step in range(1, 4):
         ox(step).start()
 
-    relays[3].wait_recv()
+    for copy in idp_copies:
+        copy.wait_recv()
+
+    def hot_of_all():
+        return jnp.concatenate([hot_dp[i] for i in range(8)], axis=1)
+
+    @pl.when(dp < PAIRS)
+    def _():
+        def hot_block(i, carry):
+            owner = lax.rem(dp + i, 8)
+            hot_dp[owner] = (token == ids_dp[i]).astype(BF)
+            return carry
+
+        lax.fori_loop(0, 8, hot_block, 0)
+
+        for i in range(8):
+            @pl.when(i != dp)
+            def _():
+                remote(q_out.at[0], q_in.at[i], q_send.at[0], q_recv.at[i], (mine, sq)).wait_recv()
+
+        tok_sum[0] = nn(hot_of_all(), q_in[...].reshape(8 * B, B)).astype(BF)
+        for step in range(1, 4):
+            @pl.when(other_x(step) == 0)
+            def _():
+                tok(step, 0).start()
+
+    for half in range(2):
+        relay(3, half).wait_recv()
     gatt[pl.ds(REACH * B, B), :] = nt(cot_all[REACH], wo[...]).astype(BF)
-    for copy in stat_copies:
-        copy.wait_recv()
+    for d in range(1, REACH + 1):
+        stat_copy(0, d).wait_recv()
 
     def oy(step):
         return remote(
@@ -339,6 +425,11 @@
         )
 
     def pass_two(p, carry):
+        @pl.when(p == 3)
+        def _():
+            for d in range(1, REACH + 1):
+                stat_copy(1, d).wait_recv()
+
         lanes = pl.ds(pl.multiple_of(p * B, B), B)
         k2 = stacked(keys[pl.ds(REACH * B, B), lanes])
         v2 = stacked(values[pl.ds(REACH * B, B), lanes])
@@ -348,8 +439,9 @@
             allowed = jnp.concatenate([reach < window_ref[2 * p], reach < window_ref[2 * p + 1]], axis=0)
 
             def spread(j):
-                a = jnp.broadcast_to(stats[d, pl.ds(16 * j + 2 * p, 1), :], (B, B))
-                b = jnp.broadcast_to(stats[d, pl.ds(16 * j + 2 * p + 1, 1), :], (B, B))
+                first = 8 * j + 2 * (p % 3)
+                a = jnp.broadcast_to(stats[p // 3, d, pl.ds(first, 1), :], (B, B))
+                b = jnp.broadcast_to(stats[p // 3, d, pl.ds(first + 1, 1), :], (B, B))
                 return jnp.concatenate([a, b], axis=0)
 
             probs = jnp.exp(jnp.where(allowed, nt(k2, q) - spread(0), -1e30))
@@ -372,7 +464,7 @@
             kv_in[dp, 0] = grad_key
             kv_in[dp, 1] = grad_value
 
-        @pl.when(p == 4)
+        @pl.when(p == 2)
         def _():
             for step in range(1, 4):
                 ox(step).wait_recv()
@@ -386,6 +478,19 @@
                 def _():
                     oy(step).start()
 
+        @pl.when((p == 5) & (dp < PAIRS))
+        def _():
+            for step in range(1, 4):
+                oy(step).wait_recv()
+            total = out_y[lax.min(y, 2)].astype(F32)
+            for step in range(3):
+                total += out_y_in[step].astype(F32)
+            out_z[...] = total.astype(BF).reshape(2, D // 8, B)
+            for i in range(2):
+                @pl.when(oz_step(i) != 0)
+                def _():
+                    oz(i).start()
+
         return carry
 
     lax.fori_loop(0, PAIRS, pass_two, 0)
@@ -398,85 +503,19 @@
         inv * (grad_normed - scaled * jnp.mean(grad_normed * scaled, axis=1, keepdims=True))
     ).astype(BF)
 
-    def tok(step, target):
-        return remote(
-            tok_sum.at[target], tok_in.at[step - 1], tok_send.at[step - 1], tok_recv.at[step - 1],
-            (dp, seq_of(target, z)),
-        )
-
-    def oz_step(i):
-        return lax.rem(2 * x + i - z + 8, 8)
-
-    def oz(i):
-        step = lax.max(oz_step(i), 1)
-        return remote(
-            out_z.at[i], out_z_in.at[step - 1], oz_send.at[i], oz_recv.at[step - 1], (dp, seq_of(x, 2 * x + i))
-        )
-
-    def oz_in(step):
-        return remote(
-            out_z.at[0], out_z_in.at[step - 1], oz_send.at[0], oz_recv.at[step - 1], (dp, seq_of(x, z))
-        )
-
-    def zs(step):
-        return remote(
-            z_out.at[other_z(step)], z_in.at[step - 1], z_send.at[step - 1], z_recv.at[step - 1],
-            (dp, seq_of(x, other_z(step))),
-        )
-
-    mine = lax.min(dp, PAIRS - 1)
-
-    def fin(step):
-        return remote(
-            final.at[mine], final.at[mine], fin_send.at[step - 1], fin_recv.at[mine], (other_dp(step), sq)
-        )
-
-    def out_fin():
-        return remote(out_final, final.at[mine], of_send.at[0], of_recv.at[0], (dp, seq_of(3, z)))
-
-    def fin_in(p):
-        return remote(final.at[p], final.at[p], fin_send.at[0], fin_recv.at[p], (p, sq))
-
-    for copy in idp_copies:
-        copy.wait_recv()
-
     @pl.when(dp < PAIRS)
     def _():
-        def hot_block(i, carry):
-            owner = lax.rem(dp + i, 8)
-            hot_dp[owner] = (token == ids_dp[i]).astype(BF)
-            return carry
-
-        lax.fori_loop(0, 8, hot_block, 0)
-
-        for i in range(8):
-            @pl.when(i != dp)
-            def _():
-                remote(q_out.at[0], q_in.at[i], q_send.at[0], q_recv.at[i], (mine, sq)).wait_recv()
-
-        hot = jnp.concatenate([hot_dp[i] for i in range(8)], axis=1)
-        tok_sum[0] = nn(hot, q_in[...].reshape(8 * B, B)).astype(BF)
         for i in range(8):
             @pl.when(i != dp)
             def _():
                 remote(kv_out.at[0], kv_in.at[i], kv_send.at[0], kv_recv.at[i], (mine, sq)).wait_recv()
-        tok_sum[1] = nn(hot, kv_in[:, 0].reshape(8 * B, B)).astype(BF)
-        tok_sum[2] = nn(hot, kv_in[:, 1].reshape(8 * B, B)).astype(BF)
+        hot_all = hot_of_all()
+        tok_sum[1] = nn(hot_all, kv_in[:, 0].reshape(8 * B, B)).astype(BF)
+        tok_sum[2] = nn(hot_all, kv_in[:, 1].reshape(8 * B, B)).astype(BF)
         for step in range(1, 4):
-            @pl.when(other_x(step) < 3)
+            @pl.when((other_x(step) > 0) & (other_x(step) < 3))
             def _():
-                tok(step, lax.min(other_x(step), 2)).start()
-
-        for step in range(1, 4):
-            oy(step).wait_recv()
-        total = out_y[lax.min(y, 2)].astype(F32)
-        for step in range(3):
-            total += out_y_in[step].astype(F32)
-        out_z[...] = total.astype(BF).reshape(2, D // 8, B)
-        for i in range(2):
-            @pl.when(oz_step(i) != 0)
-            def _():
-                oz(i).start()
+                tok(step, lax.clamp(1, other_x(step), 2)).start()
 
         @pl.when(x < 3)
         def _():
@@ -485,8 +524,8 @@
             total = tok_sum[lax.min(x, 2)].astype(F32)
             for step in range(3):
                 total += tok_in[step].astype(F32)
-            z_out[...] = tn(ntab[...], total.astype(BF)).astype(BF).reshape(8, D // 8, B)
-            for step in range(1, 8):
+            z_out[...] = nn(ntab_t[...], total.astype(BF)).astype(BF).reshape(8, D // 8, B)
+            for step in (4, 3, 5, 2, 6, 1, 7):
                 zs(step).start()
 
         @pl.when(z // 2 == x)
@@ -519,7 +558,7 @@
         def _():
             out_fin().wait_recv()
 
-        for step in range(1, 8):
+        for step in (4, 3, 5, 2, 6, 1, 7):
             fin(step).start()
 
     for p in range(PAIRS):
@@ -527,8 +566,8 @@
         def _():
             fin_in(p).wait_recv()
 
-        wg_ref[:, pl.ds(p * B, B)] = final[p].astype(F32)
-
+    relays = [relay(step, half) for step in range(REACH) for half in range(2)]
+    stat_copies = [stat_copy(part, d) for part in range(2) for d in range(1, REACH + 1)]
     for copy in id_copies + idp_copies + relays + stat_copies + [oc] + [ox(step) for step in range(1, 4)]:
         copy.wait_send()
     for p in range(PAIRS):
@@ -565,17 +604,23 @@
             fin(step).wait_send()
 
 
+def finish(gin_ref, pieces_ref, gin_out, wg_out):
+    gin_out[...] = gin_ref[...]
+    for p in range(PAIRS):
+        wg_out[:, pl.ds(p * B, B)] = pieces_ref[p].astype(F32)
+
+
 def on_device(token_ids, cotangent, table, w_query, w_key, w_value, w_out, window):
     tables = [jnp.asarray(part) for part in rope_tables()]
     vmem = pl.BlockSpec(memory_space=pltpu.VMEM)
     hbm = pl.BlockSpec(memory_space=pl.ANY)
     smem = pl.BlockSpec(memory_space=pltpu.SMEM)
     dma = pltpu.SemaphoreType.DMA
-    grad_input, weight_grads = pl.pallas_call(
+    grad_input, pieces = pl.pallas_call(
         kernel,
         out_shape=(
             jax.ShapeDtypeStruct((B, D), BF),
-            jax.ShapeDtypeStruct((D // 8, D), F32),
+            jax.ShapeDtypeStruct((PAIRS, D // 8, B), BF),
         ),
         in_specs=[vmem] + [hbm] * 6 + [smem] + [vmem] * 4,
         out_specs=(vmem, vmem),
@@ -588,6 +633,7 @@
             pltpu.VMEM((D, D), BF),
             pltpu.VMEM((D, D), BF),
             pltpu.VMEM((D, D), BF),
+            pltpu.VMEM((D, VOCAB), BF),
             pltpu.VMEM((VOCAB, D), BF),
             pltpu.VMEM((VOCAB, D), BF),
             pltpu.VMEM((VOCAB, D), BF),
@@ -607,7 +653,7 @@
             pltpu.VMEM((B, D), BF),
             pltpu.VMEM((B, D), BF),
             pltpu.VMEM((B, B), F32),
-            pltpu.VMEM((REACH + 1, 32, B), F32),
+            pltpu.VMEM((2, REACH + 1, 16, B), F32),
             pltpu.VMEM((2 * B, SPAN), BF),
             pltpu.VMEM((2 * B, SPAN), BF),
             pltpu.VMEM((8, VOCAB, B), BF),
@@ -619,7 +665,6 @@
             pltpu.VMEM((3, VOCAB, B), BF),
             pltpu.VMEM((8, D // 8, B), BF),
             pltpu.VMEM((7, D // 8, B), BF),
-            pltpu.VMEM((PAIRS, D // 8, B), BF),
             pltpu.VMEM((2, 4, 3, D // 4, B), BF),
             pltpu.VMEM((4, 3, D // 4, B), BF),
             pltpu.VMEM((4, 3, D // 4, B), BF),
@@ -629,13 +674,22 @@
             pltpu.VMEM((2, D // 8, B), BF),
             pltpu.VMEM((7, D // 8, B), BF),
             pltpu.VMEM((D // 8, B), BF),
-            dma((6,)), dma((8,)), dma((8,)), dma((7,)), dma((7,)), dma((4,)), dma((4,)), dma((4,)), dma((4,)),
+            dma((6,)), dma((8,)), dma((8,)), dma((7,)), dma((7,)), dma((8,)), dma((8,)), dma((8,)), dma((8,)),
             dma((PAIRS,)), dma((8,)), dma((PAIRS,)), dma((8,)), dma((3,)), dma((3,)), dma((7,)), dma((7,)),
             dma((7,)), dma((PAIRS,)),
             dma((1,)), dma((1,)), dma((3,)), dma((3,)), dma((3,)), dma((3,)), dma((2,)), dma((7,)), dma((1,)), dma((1,)),
         ],
         compiler_params=pltpu.CompilerParams(collective_id=0, has_side_effects=True),
     )(token_ids, cotangent[0], table, w_query, w_key, w_value, w_out, window, *tables)
+    grad_input, weight_grads = pl.pallas_call(
+        finish,
+        out_shape=(
+            jax.ShapeDtypeStruct((B, D), BF),
+            jax.ShapeDtypeStruct((D // 8, D), F32),
+        ),
+        in_specs=[vmem, vmem],
+        out_specs=(vmem, vmem),
+    )(grad_input, pieces)
     return (grad_input[None], weight_grads)
 
 

time: 74 us -> 75.6 us (1.022)
  the two profiles are of different devices: /device:TPU:1 before, /device:TPU:5 now
where the time goes in v4:
time: 75.6 us; the launch traced here: 75.5 us
  Pallas kernels  74.9 us (99%)
    pallas_call x1, Pallas kernels, on_device(): pl.pallas_call(kernel, out_shape=(jax.ShapeDtypeStruct((B, D), BF), jax.S...  73.1 us
    pallas_call x1, Pallas kernels, on_device(): pl.pallas_call(finish, out_shape=(jax.ShapeDtypeStruct((B, D), BF), jax.S...  1.8 us

profile of v4, /device:TPU:5, one launch (start us, length us, event | category | flops | bytes accessed | tf_op | source)
XLA Modules:
  0.0 75.5 jit_solution(8007826932106479300)
XLA Ops:
  0.6 73.1 %shard_map.131 = (bf16[128,768]{1,0:T(8,128)(2,1)}, bf16[6,96,128]{2,1,0:T(8,128)(2,1)}) custom-call(s32[1,128]{1,0:T(1,128)} %ids_ref.1, bf16[128,768]{1,0:T(8,128)(2,1)} %bitcast.2, bf16[256,768]{1,0:T(8,128)(2,1)} %table_hbm.1, bf16[768,768]{1,0:T(8,128)(2,1)} %wq_hbm.1, bf16[768,768]{1,0:T(8,128)(2,1)} %wk_hbm.1, bf16[768,768]{1,0:T(8,128)(2,1)} %wv_hbm.1, ...), custom_call_target="tpu_custom_call" | custom-call | tf_op jit(solution)/shard_map/pallas_call | solution.py:619
  73.7 1.8 %shard_map.132 = (bf16[128,768]{1,0:T(8,128)(2,1)}, f32[96,768]{1,0:T(8,128)}) custom-call(bf16[128,768]{1,0:T(8,128)(2,1)} %get-tuple-element.6.gin_ref, bf16[6,96,128]{2,1,0:T(8,128)(2,1)} %get-tuple-element.7.pieces_ref), custom_call_target="tpu_custom_call" | custom-call | tf_op jit(solution)/shard_map/pallas_call | solution.py:684

commit v5 on v4

--- a/solution.py
+++ b/solution.py
@@ -251,7 +251,7 @@
         at = REACH * part + d - 1
         return remote(stats.at[part, 0], stats.at[part, d], st_send.at[at], st_recv.at[at], (dp, shift(-d)))
 
-    def pass_one(p, carry):
+    def pass_one(p):
         lanes = pl.ds(pl.multiple_of(p * B, B), B)
         k, v = keys[:, lanes], values[:, lanes]
         scores = nt(stacked(query[pl.ds(0, B), lanes]), k)
@@ -275,39 +275,44 @@
         got = unrope(grad_query, own_cos, own_sin).astype(BF)
         gq[:, lanes] = got
 
-        @pl.when(p != dp)
-        def _():
-            q_out[p] = got
-            q_copy(p).start()
-
-        @pl.when(p == dp)
-        def _():
-            q_in[dp] = got
-
+        q_out[p] = got
         held = statc[...]
         for j, stat in enumerate((top + jnp.log(whole), row_term)):
-            first = 16 * (p // 3) + 8 * j + 2 * (p % 3)
+            first = 16 * (p // 4) + 8 * j + 2 * (p % 4)
             held = jnp.where(lane_one == first, stat[:B], held)
             held = jnp.where(lane_one == first + 1, stat[B:], held)
         statc[...] = held
 
-        @pl.when(p == 1)
+
+    def send_q(p):
+        @pl.when(p != dp)
+        def _():
+            q_copy(p).start()
+
+        @pl.when(p == dp)
+        def _():
+            q_in[dp] = q_out[p]
+
+    def pass_one_pairs(i, carry):
+        pass_one(2 * i)
+        pass_one(2 * i + 1)
+        send_q(2 * i)
+        send_q(2 * i + 1)
+
+        @pl.when(i == 0)
         def _():
             forward(2, 1)
 
-        @pl.when(p == 2)
+        @pl.when(i == 1)
         def _():
             stats[0, 0] = statc[...].T[:16]
             for d in range(REACH, 0, -1):
                 stat_copy(0, d).start()
-
-        @pl.when(p == 3)
-        def _():
             forward(3, 0)
 
         return carry
 
-    lax.fori_loop(0, PAIRS, pass_one, 0)
+    lax.fori_loop(0, PAIRS // 2, pass_one_pairs, 0)
 
     stats[1, 0] = statc[...].T[16:32]
     for d in range(REACH, 0, -1):
@@ -424,12 +429,8 @@
             (other_y(step) * 2 + c, sq),
         )
 
-    def pass_two(p, carry):
-        @pl.when(p == 3)
-        def _():
-            for d in range(1, REACH + 1):
-                stat_copy(1, d).wait_recv()
-
+    def pass_two(i, slot):
+        p = 2 * i + slot
         lanes = pl.ds(pl.multiple_of(p * B, B), B)
         k2 = stacked(keys[pl.ds(REACH * B, B), lanes])
         v2 = stacked(values[pl.ds(REACH * B, B), lanes])
@@ -439,61 +440,57 @@
             allowed = jnp.concatenate([reach < window_ref[2 * p], reach < window_ref[2 * p + 1]], axis=0)
 
             def spread(j):
-                first = 8 * j + 2 * (p % 3)
-                a = jnp.broadcast_to(stats[p // 3, d, pl.ds(first, 1), :], (B, B))
-                b = jnp.broadcast_to(stats[p // 3, d, pl.ds(first + 1, 1), :], (B, B))
+                first = 8 * j + 2 * (p % 4)
+                a = jnp.broadcast_to(stats[p // 4, d, pl.ds(first, 1), :], (B, B))
+                b = jnp.broadcast_to(stats[p // 4, d, pl.ds(first + 1, 1), :], (B, B))
                 return jnp.concatenate([a, b], axis=0)
 
             probs = jnp.exp(jnp.where(allowed, nt(k2, q) - spread(0), -1e30))
             ds = probs * (nt(v2, g) - spread(1))
-            probs_s[:, pl.ds(d * B, B)] = probs.astype(BF)
-            ds_s[:, pl.ds(d * B, B)] = ds.astype(BF)
-        grad_value = picked(nn(probs_s[...], gatt[:, lanes])).astype(BF)
-        grad_key = unrope(picked(nn(ds_s[...], query[:, lanes])), own_cos, own_sin).astype(BF)
+            probs_s[slot, :, pl.ds(d * B, B)] = probs.astype(BF)
+            ds_s[slot, :, pl.ds(d * B, B)] = ds.astype(BF)
+        grad_value = picked(nn(probs_s[slot], gatt[:, lanes])).astype(BF)
+        grad_key = unrope(picked(nn(ds_s[slot], query[:, lanes])), own_cos, own_sin).astype(BF)
         gv[:, lanes] = grad_value
         gk[:, lanes] = grad_key
 
+        kv_out[p, 0] = grad_key
+        kv_out[p, 1] = grad_value
+
+    def send_kv(p):
         @pl.when(p != dp)
         def _():
-            kv_out[p, 0] = grad_key
-            kv_out[p, 1] = grad_value
             kv_copy(p).start()
 
         @pl.when(p == dp)
         def _():
-            kv_in[dp, 0] = grad_key
-            kv_in[dp, 1] = grad_value
-
-        @pl.when(p == 2)
-        def _():
-            for step in range(1, 4):
-                ox(step).wait_recv()
-            for row in range(3):
-                total = out_x[x, row].astype(F32)
-                for step in range(3):
-                    total += out_x_in[step, row].astype(F32)
-                out_y[row] = total.astype(BF)
-            for step in range(1, 4):
-                @pl.when(other_y(step) < 3)
-                def _():
-                    oy(step).start()
-
-        @pl.when((p == 5) & (dp < PAIRS))
-        def _():
-            for step in range(1, 4):
-                oy(step).wait_recv()
-            total = out_y[lax.min(y, 2)].astype(F32)
-            for step in range(3):
-                total += out_y_in[step].astype(F32)
-            out_z[...] = total.astype(BF).reshape(2, D // 8, B)
-            for i in range(2):
-                @pl.when(oz_step(i) != 0)
-                def _():
-                    oz(i).start()
-
+            kv_in[dp] = kv_out[p]
+
+    def pass_two_pairs(i, carry):
+        @pl.when(i == 2)
+        def _():
+            for d in range(1, REACH + 1):
+                stat_copy(1, d).wait_recv()
+
+        pass_two(i, 0)
+        pass_two(i, 1)
+        send_kv(2 * i)
+        send_kv(2 * i + 1)
         return carry
 
-    lax.fori_loop(0, PAIRS, pass_two, 0)
+    lax.fori_loop(0, PAIRS // 2, pass_two_pairs, 0)
+
+    for step in range(1, 4):
+        ox(step).wait_recv()
+    for row in range(3):
+        total = out_x[x, row].astype(F32)
+        for step in range(3):
+            total += out_x_in[step, row].astype(F32)
+        out_y[row] = total.astype(BF)
+    for step in range(1, 4):
+        @pl.when(other_y(step) < 3)
+        def _():
+            oy(step).start()
 
     grad_normed = nt(gq[...], wq[...]) + nt(gk[...], wk[...]) + nt(gv[...], wv[...])
     own = emb[...]
@@ -516,6 +513,17 @@
             @pl.when((other_x(step) > 0) & (other_x(step) < 3))
             def _():
                 tok(step, lax.clamp(1, other_x(step), 2)).start()
+
+        for step in range(1, 4):
+            oy(step).wait_recv()
+        total = out_y[lax.min(y, 2)].astype(F32)
+        for step in range(3):
+            total += out_y_in[step].astype(F32)
+        out_z[...] = total.astype(BF).reshape(2, D // 8, B)
+        for i in range(2):
+            @pl.when(oz_step(i) != 0)
+            def _():
+                oz(i).start()
 
         @pl.when(x < 3)
         def _():
@@ -654,8 +662,8 @@
             pltpu.VMEM((B, D), BF),
             pltpu.VMEM((B, B), F32),
             pltpu.VMEM((2, REACH + 1, 16, B), F32),
-            pltpu.VMEM((2 * B, SPAN), BF),
-            pltpu.VMEM((2 * B, SPAN), BF),
+            pltpu.VMEM((2, 2 * B, SPAN), BF),
+            pltpu.VMEM((2, 2 * B, SPAN), BF),
             pltpu.VMEM((8, VOCAB, B), BF),
             pltpu.VMEM((PAIRS, B, B), BF),
             pltpu.VMEM((PAIRS, 2, B, B), BF),

time: 75.6 us -> 68.4 us (0.905)
  the two profiles are of different devices: /device:TPU:5 before, /device:TPU:1 now
where the time goes in v5:
time: 68.4 us; the launch traced here: 68.3 us
  Pallas kernels  67.6 us (99%)
    pallas_call x1, Pallas kernels, on_device(): pl.pallas_call(kernel, out_shape=(jax.ShapeDtypeStruct((B, D), BF), jax.S...  65.8 us
    pallas_call x1, Pallas kernels, on_device(): pl.pallas_call(finish, out_shape=(jax.ShapeDtypeStruct((B, D), BF), jax.S...  1.8 us

profile of v5, /device:TPU:1, one launch (start us, length us, event | category | flops | bytes accessed | tf_op | source)
XLA Modules:
  0.0 68.3 jit_solution(1389215759591861922)
XLA Ops:
  0.6 65.8 %shard_map.131 = (bf16[128,768]{1,0:T(8,128)(2,1)}, bf16[6,96,128]{2,1,0:T(8,128)(2,1)}) custom-call(s32[1,128]{1,0:T(1,128)} %ids_ref.1, bf16[128,768]{1,0:T(8,128)(2,1)} %bitcast.2, bf16[256,768]{1,0:T(8,128)(2,1)} %table_hbm.1, bf16[768,768]{1,0:T(8,128)(2,1)} %wq_hbm.1, bf16[768,768]{1,0:T(8,128)(2,1)} %wk_hbm.1, bf16[768,768]{1,0:T(8,128)(2,1)} %wv_hbm.1, ...), custom_call_target="tpu_custom_call" | custom-call | tf_op jit(solution)/shard_map/pallas_call | solution.py:627
  66.5 1.8 %shard_map.132 = (bf16[128,768]{1,0:T(8,128)(2,1)}, f32[96,768]{1,0:T(8,128)}) custom-call(bf16[128,768]{1,0:T(8,128)(2,1)} %get-tuple-element.6.gin_ref, bf16[6,96,128]{2,1,0:T(8,128)(2,1)} %get-tuple-element.7.pieces_ref), custom_call_target="tpu_custom_call" | custom-call | tf_op jit(solution)/shard_map/pallas_call | solution.py:692

commit v6 on v5

--- a/solution.py
+++ b/solution.py
@@ -251,7 +251,11 @@
         at = REACH * part + d - 1
         return remote(stats.at[part, 0], stats.at[part, d], st_send.at[at], st_recv.at[at], (dp, shift(-d)))
 
-    def pass_one(p):
+    def pair_of(i, slot):
+        return 3 + i if slot else 2 - i
+
+    def pass_one(i, slot):
+        p = pair_of(i, slot)
         lanes = pl.ds(pl.multiple_of(p * B, B), B)
         k, v = keys[:, lanes], values[:, lanes]
         scores = nt(stacked(query[pl.ds(0, B), lanes]), k)
@@ -278,7 +282,7 @@
         q_out[p] = got
         held = statc[...]
         for j, stat in enumerate((top + jnp.log(whole), row_term)):
-            first = 16 * (p // 4) + 8 * j + 2 * (p % 4)
+            first = 16 * (i // 2) + 8 * j + 2 * (2 * (i % 2) + slot)
             held = jnp.where(lane_one == first, stat[:B], held)
             held = jnp.where(lane_one == first + 1, stat[B:], held)
         statc[...] = held
@@ -293,11 +297,48 @@
         def _():
             q_in[dp] = q_out[p]
 
+    def out_terms(first, count, blocks):
+        att_t = att[:, pl.ds(first, count)].T
+
+        def one_pair(p, carry):
+            lanes = pl.ds(pl.multiple_of(p * B, B), B)
+            got = nn(att_t, cot_all[0, :, lanes]).astype(BF)
+            for block in blocks:
+                start = block * (D // 4) - first
+                out_term[p % 2, block, p // 2] = got[start : start + D // 4]
+            return carry
+
+        lax.fori_loop(0, PAIRS, one_pair, 0)
+        for block in blocks:
+            oc(block).start()
+
+    def oc(block):
+        return remote(
+            out_term.at[1 - c, block], out_core.at[block], oc_send.at[block], oc_recv.at[block],
+            (y * 2 + 1 - c, sq),
+        )
+
+    def ox(step):
+        return remote(
+            out_x.at[other_x(step)], out_x_in.at[step - 1], ox_send.at[step - 1], ox_recv.at[step - 1],
+            (dp, seq_of(other_x(step), z)),
+        )
+
+    def out_core_sum(blocks):
+        for block in blocks:
+            oc(block).wait_recv()
+            out_x[block] = (out_term[c, block].astype(F32) + out_core[block].astype(F32)).astype(BF)
+        for step in range(1, 4):
+            for block in blocks:
+                @pl.when(other_x(step) == block)
+                def _():
+                    ox(step).start()
+
     def pass_one_pairs(i, carry):
-        pass_one(2 * i)
-        pass_one(2 * i + 1)
-        send_q(2 * i)
-        send_q(2 * i + 1)
+        for slot in range(2):
+            pass_one(i, slot)
+        for slot in range(2):
+            send_q(pair_of(i, slot))
 
         @pl.when(i == 0)
         def _():
@@ -309,6 +350,7 @@
             for d in range(REACH, 0, -1):
                 stat_copy(0, d).start()
             forward(3, 0)
+            out_terms(B, 4 * B, (1, 2))
 
         return carry
 
@@ -318,24 +360,13 @@
     for d in range(REACH, 0, -1):
         stat_copy(1, d).start()
     forward(3, 1)
+    out_terms(0, D, (0, 3))
+    out_core_sum((1, 2))
 
     ntab_t[...] = ntab[...].T
     emb[...] = nn(hot[pl.ds(REACH * B, B), :], table[...])
     select(qtab, query, (REACH + 1) * B, B, REACH * B, True, HEAD_DIM ** (-0.5))
 
-    att_t = att[...].T
-
-    def out_terms(p, carry):
-        lanes = pl.ds(pl.multiple_of(p * B, B), B)
-        got = nn(att_t, cot_all[0, :, lanes]).astype(BF)
-        for block in range(4):
-            out_term[p % 2, block, p // 2] = got[block * 192 : (block + 1) * 192]
-        return carry
-
-    lax.fori_loop(0, PAIRS, out_terms, 0)
-    oc = remote(out_term.at[1 - c], out_core, oc_send.at[0], oc_recv.at[0], (y * 2 + 1 - c, sq))
-    oc.start()
-
     for d in range(1, 4):
         gatt[pl.ds(d * B, B), :] = nt(cot_all[d], wo[...]).astype(BF)
 
@@ -359,37 +390,32 @@
             out_z.at[0], out_z_in.at[step - 1], oz_send.at[0], oz_recv.at[step - 1], (dp, seq_of(x, z))
         )
 
-    def zs(step):
-        return remote(
-            z_out.at[other_z(step)], z_in.at[step - 1], z_send.at[step - 1], z_recv.at[step - 1],
+    part_rows = D // 16
+
+    def zs(step, half):
+        rows = pl.ds(half * part_rows, part_rows)
+        at = 7 * half + step - 1
+        return remote(
+            z_out.at[other_z(step), rows], z_in.at[step - 1, rows], z_send.at[at], z_recv.at[at],
             (dp, seq_of(x, other_z(step))),
         )
 
     mine = lax.min(dp, PAIRS - 1)
 
-    def fin(step):
-        return remote(
-            final.at[mine], final.at[mine], fin_send.at[step - 1], fin_recv.at[mine], (other_dp(step), sq)
+    def fin(step, half):
+        part = final.at[mine, pl.ds(half * part_rows, part_rows)]
+        return remote(
+            part, part, fin_send.at[7 * half + step - 1], fin_recv.at[half, mine], (other_dp(step), sq)
         )
 
     def out_fin():
         return remote(out_final, final.at[mine], of_send.at[0], of_recv.at[0], (dp, seq_of(3, z)))
 
-    def fin_in(p):
-        return remote(final.at[p], final.at[p], fin_send.at[0], fin_recv.at[p], (p, sq))
-
-    oc.wait_recv()
-    for block in range(4):
-        out_x[block] = (out_term[c, block].astype(F32) + out_core[block].astype(F32)).astype(BF)
-
-    def ox(step):
-        return remote(
-            out_x.at[other_x(step)], out_x_in.at[step - 1], ox_send.at[step - 1], ox_recv.at[step - 1],
-            (dp, seq_of(other_x(step), z)),
-        )
-
-    for step in range(1, 4):
-        ox(step).start()
+    def fin_in(p, half):
+        part = final.at[p, pl.ds(half * part_rows, part_rows)]
+        return remote(part, part, fin_send.at[0], fin_recv.at[half, p], (p, sq))
+
+    out_core_sum((0, 3))
 
     for copy in idp_copies:
         copy.wait_recv()
@@ -430,7 +456,7 @@
         )
 
     def pass_two(i, slot):
-        p = 2 * i + slot
+        p = pair_of(i, slot)
         lanes = pl.ds(pl.multiple_of(p * B, B), B)
         k2 = stacked(keys[pl.ds(REACH * B, B), lanes])
         v2 = stacked(values[pl.ds(REACH * B, B), lanes])
@@ -440,9 +466,9 @@
             allowed = jnp.concatenate([reach < window_ref[2 * p], reach < window_ref[2 * p + 1]], axis=0)
 
             def spread(j):
-                first = 8 * j + 2 * (p % 4)
-                a = jnp.broadcast_to(stats[p // 4, d, pl.ds(first, 1), :], (B, B))
-                b = jnp.broadcast_to(stats[p // 4, d, pl.ds(first + 1, 1), :], (B, B))
+                first = 8 * j + 2 * (2 * (i % 2) + slot)
+                a = jnp.broadcast_to(stats[i // 2, d, pl.ds(first, 1), :], (B, B))
+                b = jnp.broadcast_to(stats[i // 2, d, pl.ds(first + 1, 1), :], (B, B))
                 return jnp.concatenate([a, b], axis=0)
 
             probs = jnp.exp(jnp.where(allowed, nt(k2, q) - spread(0), -1e30))
@@ -472,10 +498,10 @@
             for d in range(1, REACH + 1):
                 stat_copy(1, d).wait_recv()
 
-        pass_two(i, 0)
-        pass_two(i, 1)
-        send_kv(2 * i)
-        send_kv(2 * i + 1)
+        for slot in range(2):
+            pass_two(i, slot)
+        for slot in range(2):
+            send_kv(pair_of(i, slot))
         return carry
 
     lax.fori_loop(0, PAIRS // 2, pass_two_pairs, 0)
@@ -508,11 +534,16 @@
                 remote(kv_out.at[0], kv_in.at[i], kv_send.at[0], kv_recv.at[i], (mine, sq)).wait_recv()
         hot_all = hot_of_all()
         tok_sum[1] = nn(hot_all, kv_in[:, 0].reshape(8 * B, B)).astype(BF)
+        for step in range(1, 4):
+            @pl.when(other_x(step) == 1)
+            def _():
+                tok(step, 1).start()
+
         tok_sum[2] = nn(hot_all, kv_in[:, 1].reshape(8 * B, B)).astype(BF)
         for step in range(1, 4):
-            @pl.when((other_x(step) > 0) & (other_x(step) < 3))
-            def _():
-                tok(step, lax.clamp(1, other_x(step), 2)).start()
+            @pl.when(other_x(step) == 2)
+            def _():
+                tok(step, 2).start()
 
         for step in range(1, 4):
             oy(step).wait_recv()
@@ -533,8 +564,9 @@
             for step in range(3):
                 total += tok_in[step].astype(F32)
             z_out[...] = nn(ntab_t[...], total.astype(BF)).astype(BF).reshape(8, D // 8, B)
-            for step in (4, 3, 5, 2, 6, 1, 7):
-                zs(step).start()
+            for half in range(2):
+                for step in (4, 3, 5, 2, 6, 1, 7):
+                    zs(step, half).start()
 
         @pl.when(z // 2 == x)
         def _():
@@ -555,28 +587,36 @@
 
         @pl.when(x < 3)
         def _():
-            for step in range(1, 8):
-                zs(step).wait_recv()
-            total = z_out[z].astype(F32)
-            for step in range(7):
-                total += z_in[step].astype(F32)
-            final[mine] = total.astype(BF)
-
-        @pl.when((x == 3) & (z < 6))
-        def _():
-            out_fin().wait_recv()
-
-        for step in (4, 3, 5, 2, 6, 1, 7):
-            fin(step).start()
+            for half in range(2):
+                rows = pl.ds(half * part_rows, part_rows)
+                for step in range(1, 8):
+                    zs(step, half).wait_recv()
+                total = z_out[z, rows].astype(F32)
+                for step in range(7):
+                    total += z_in[step, rows].astype(F32)
+                final[mine, rows] = total.astype(BF)
+                for step in (4, 3, 5, 2, 6, 1, 7):
+                    fin(step, half).start()
+
+        @pl.when(x == 3)
+        def _():
+            @pl.when(z < 6)
+            def _():
+                out_fin().wait_recv()
+
+            for half in range(2):
+                for step in (4, 3, 5, 2, 6, 1, 7):
+                    fin(step, half).start()
 
     for p in range(PAIRS):
         @pl.when(dp != p)
         def _():
-            fin_in(p).wait_recv()
+            for half in range(2):
+                fin_in(p, half).wait_recv()
 
     relays = [relay(step, half) for step in range(REACH) for half in range(2)]
     stat_copies = [stat_copy(part, d) for part in range(2) for d in range(1, REACH + 1)]
-    for copy in id_copies + idp_copies + relays + stat_copies + [oc] + [ox(step) for step in range(1, 4)]:
+    for copy in id_copies + idp_copies + relays + stat_copies + [oc(block) for block in range(4)] + [ox(step) for step in range(1, 4)]:
         copy.wait_send()
     for p in range(PAIRS):
         @pl.when(p != dp)
@@ -601,15 +641,17 @@
 
         @pl.when(x < 3)
         def _():
+            for half in range(2):
+                for step in range(1, 8):
+                    zs(step, half).wait_send()
+
+        @pl.when((z // 2 == x) & (x < 3))
+        def _():
+            out_fin().wait_send()
+
+        for half in range(2):
             for step in range(1, 8):
-                zs(step).wait_send()
-
-        @pl.when((z // 2 == x) & (x < 3))
-        def _():
-            out_fin().wait_send()
-
-        for step in range(1, 8):
-            fin(step).wait_send()
+                fin(step, half).wait_send()
 
 
 def finish(gin_ref, pieces_ref, gin_out, wg_out):
@@ -683,9 +725,9 @@
             pltpu.VMEM((7, D // 8, B), BF),
             pltpu.VMEM((D // 8, B), BF),
             dma((6,)), dma((8,)), dma((8,)), dma((7,)), dma((7,)), dma((8,)), dma((8,)), dma((8,)), dma((8,)),
-            dma((PAIRS,)), dma((8,)), dma((PAIRS,)), dma((8,)), dma((3,)), dma((3,)), dma((7,)), dma((7,)),
-            dma((7,)), dma((PAIRS,)),
-            dma((1,)), dma((1,)), dma((3,)), dma((3,)), dma((3,)), dma((3,)), dma((2,)), dma((7,)), dma((1,)), dma((1,)),
+            dma((PAIRS,)), dma((8,)), dma((PAIRS,)), dma((8,)), dma((3,)), dma((3,)), dma((14,)), dma((14,)),
+            dma((14,)), dma((2, PAIRS)),
+            dma((4,)), dma((4,)), dma((3,)), dma((3,)), dma((3,)), dma((3,)), dma((2,)), dma((7,)), dma((1,)), dma((1,)),
         ],
         compiler_params=pltpu.CompilerParams(collective_id=0, has_side_effects=True),
     )(token_ids, cotangent[0], table, w_query, w_key, w_value, w_out, window, *tables)

time: 68.4 us -> 65 us (0.950)
  Pallas kernels: 67.6 us -> 63.9 us
    pallas_call x1, Pallas kernels: 65.8 us -> 62.1 us  [on_device(): pl.pallas_call(kernel, out_shape=(jax.ShapeDtypeStruct((B, D), BF), jax.S...]
where the time goes in v6:
time: 65 us; the launch traced here: 64.6 us
  Pallas kernels  63.9 us (98%)
    pallas_call x1, Pallas kernels, on_device(): pl.pallas_call(kernel, out_shape=(jax.ShapeDtypeStruct((B, D), BF), jax.S...  62.1 us
    pallas_call x1, Pallas kernels, on_device(): pl.pallas_call(finish, out_shape=(jax.ShapeDtypeStruct((B, D), BF), jax.S...  1.8 us

profile of v6, /device:TPU:1, one launch (start us, length us, event | category | flops | bytes accessed | tf_op | source)
XLA Modules:
  0.0 64.6 jit_solution(5609760118378306213)
XLA Ops:
  0.6 62.1 %shard_map.131 = (bf16[128,768]{1,0:T(8,128)(2,1)}, bf16[6,96,128]{2,1,0:T(8,128)(2,1)}) custom-call(s32[1,128]{1,0:T(1,128)} %ids_ref.1, bf16[128,768]{1,0:T(8,128)(2,1)} %bitcast.2, bf16[256,768]{1,0:T(8,128)(2,1)} %table_hbm.1, bf16[768,768]{1,0:T(8,128)(2,1)} %wq_hbm.1, bf16[768,768]{1,0:T(8,128)(2,1)} %wk_hbm.1, bf16[768,768]{1,0:T(8,128)(2,1)} %wv_hbm.1, ...), custom_call_target="tpu_custom_call" | custom-call | tf_op jit(solution)/shard_map/pallas_call | solution.py:669
  62.8 1.8 %shard_map.132 = (bf16[128,768]{1,0:T(8,128)(2,1)}, f32[96,768]{1,0:T(8,128)}) custom-call(bf16[128,768]{1,0:T(8,128)(2,1)} %get-tuple-element.6.gin_ref, bf16[6,96,128]{2,1,0:T(8,128)(2,1)} %get-tuple-element.7.pieces_ref), custom_call_target="tpu_custom_call" | custom-call | tf_op jit(solution)/shard_map/pallas_call | solution.py:734

commit v7 on v6

--- a/solution.py
+++ b/solution.py
@@ -241,15 +241,24 @@
     own_sin = sinv[pl.ds(REACH * B, B), :]
     statc[...] = jnp.zeros_like(statc)
 
+    def owner_of(p):
+        return p + 3 * jnp.where(p == 3, 1, 0)
+
+    owns_tokens = (dp != 3) & (dp != 7)
+    owned = jnp.where(dp == 6, 3, lax.min(dp, PAIRS - 1))
+
     def q_copy(p):
-        return remote(q_out.at[p], q_in.at[dp], q_send.at[p], q_recv.at[dp], (p, sq))
+        return remote(q_out.at[p], q_in.at[dp], q_send.at[p], q_recv.at[dp], (owner_of(p), sq))
 
     def kv_copy(p):
-        return remote(kv_out.at[p], kv_in.at[dp], kv_send.at[p], kv_recv.at[dp], (p, sq))
+        return remote(kv_out.at[p], kv_in.at[dp], kv_send.at[p], kv_recv.at[dp], (owner_of(p), sq))
 
     def stat_copy(part, d):
         at = REACH * part + d - 1
-        return remote(stats.at[part, 0], stats.at[part, d], st_send.at[at], st_recv.at[at], (dp, shift(-d)))
+        rows = pl.ds(0, 8 if part else 16)
+        return remote(
+            stats.at[part, 0, rows], stats.at[part, d, rows], st_send.at[at], st_recv.at[at], (dp, shift(-d))
+        )
 
     def pair_of(i, slot):
         return 3 + i if slot else 2 - i
@@ -282,18 +291,18 @@
         q_out[p] = got
         held = statc[...]
         for j, stat in enumerate((top + jnp.log(whole), row_term)):
-            first = 16 * (i // 2) + 8 * j + 2 * (2 * (i % 2) + slot)
+            first = 16 * (i // 2) + (8 - 4 * (i // 2)) * j + 2 * (2 * (i % 2) + slot)
             held = jnp.where(lane_one == first, stat[:B], held)
             held = jnp.where(lane_one == first + 1, stat[B:], held)
         statc[...] = held
 
 
     def send_q(p):
-        @pl.when(p != dp)
+        @pl.when(owner_of(p) != dp)
         def _():
             q_copy(p).start()
 
-        @pl.when(p == dp)
+        @pl.when(owner_of(p) == dp)
         def _():
             q_in[dp] = q_out[p]
 
@@ -356,10 +365,10 @@
 
     lax.fori_loop(0, PAIRS // 2, pass_one_pairs, 0)
 
-    stats[1, 0] = statc[...].T[16:32]
+    forward(3, 1)
+    stats[1, 0, pl.ds(0, 8)] = statc[...].T[16:24]
     for d in range(REACH, 0, -1):
         stat_copy(1, d).start()
-    forward(3, 1)
     out_terms(0, D, (0, 3))
     out_core_sum((1, 2))
 
@@ -401,11 +410,12 @@
         )
 
     mine = lax.min(dp, PAIRS - 1)
+    slot_here = jnp.where(x == 3, mine, owned)
 
     def fin(step, half):
-        part = final.at[mine, pl.ds(half * part_rows, part_rows)]
-        return remote(
-            part, part, fin_send.at[7 * half + step - 1], fin_recv.at[half, mine], (other_dp(step), sq)
+        part = final.at[slot_here, pl.ds(half * part_rows, part_rows)]
+        return remote(
+            part, part, fin_send.at[7 * half + step - 1], fin_recv.at[half, slot_here], (other_dp(step), sq)
         )
 
     def out_fin():
@@ -423,7 +433,7 @@
     def hot_of_all():
         return jnp.concatenate([hot_dp[i] for i in range(8)], axis=1)
 
-    @pl.when(dp < PAIRS)
+    @pl.when(owns_tokens)
     def _():
         def hot_block(i, carry):
             owner = lax.rem(dp + i, 8)
@@ -466,7 +476,7 @@
             allowed = jnp.concatenate([reach < window_ref[2 * p], reach < window_ref[2 * p + 1]], axis=0)
 
             def spread(j):
-                first = 8 * j + 2 * (2 * (i % 2) + slot)
+                first = (8 - 4 * (i // 2)) * j + 2 * (2 * (i % 2) + slot)
                 a = jnp.broadcast_to(stats[i // 2, d, pl.ds(first, 1), :], (B, B))
                 b = jnp.broadcast_to(stats[i // 2, d, pl.ds(first + 1, 1), :], (B, B))
                 return jnp.concatenate([a, b], axis=0)
@@ -484,11 +494,11 @@
         kv_out[p, 1] = grad_value
 
     def send_kv(p):
-        @pl.when(p != dp)
+        @pl.when(owner_of(p) != dp)
         def _():
             kv_copy(p).start()
 
-        @pl.when(p == dp)
+        @pl.when(owner_of(p) == dp)
         def _():
             kv_in[dp] = kv_out[p]
 
@@ -526,7 +536,7 @@
         inv * (grad_normed - scaled * jnp.mean(grad_normed * scaled, axis=1, keepdims=True))
     ).astype(BF)
 
-    @pl.when(dp < PAIRS)
+    @pl.when(owns_tokens)
     def _():
         for i in range(8):
             @pl.when(i != dp)
@@ -545,6 +555,8 @@
             def _():
                 tok(step, 2).start()
 
+    @pl.when(dp < PAIRS)
+    def _():
         for step in range(1, 4):
             oy(step).wait_recv()
         total = out_y[lax.min(y, 2)].astype(F32)
@@ -556,6 +568,8 @@
             def _():
                 oz(i).start()
 
+    @pl.when(owns_tokens)
+    def _():
         @pl.when(x < 3)
         def _():
             for step in range(1, 4):
@@ -568,6 +582,8 @@
                 for step in (4, 3, 5, 2, 6, 1, 7):
                     zs(step, half).start()
 
+    @pl.when(dp < PAIRS)
+    def _():
         @pl.when(z // 2 == x)
         def _():
             for step in range(1, 8):
@@ -585,6 +601,8 @@
             def _():
                 final[mine] = out_final[...]
 
+    @pl.when(owns_tokens)
+    def _():
         @pl.when(x < 3)
         def _():
             for half in range(2):
@@ -594,10 +612,12 @@
                 total = z_out[z, rows].astype(F32)
                 for step in range(7):
                     total += z_in[step, rows].astype(F32)
-                final[mine, rows] = total.astype(BF)
+                final[owned, rows] = total.astype(BF)
                 for step in (4, 3, 5, 2, 6, 1, 7):
                     fin(step, half).start()
 
+    @pl.when(dp < PAIRS)
+    def _():
         @pl.when(x == 3)
         def _():
             @pl.when(z < 6)
@@ -609,7 +629,7 @@
                     fin(step, half).start()
 
     for p in range(PAIRS):
-        @pl.when(dp != p)
+        @pl.when(dp != (p if p != 3 else jnp.where(x == 3, 3, 6)))
         def _():
             for half in range(2):
                 fin_in(p, half).wait_recv()
@@ -619,7 +639,7 @@
     for copy in id_copies + idp_copies + relays + stat_copies + [oc(block) for block in range(4)] + [ox(step) for step in range(1, 4)]:
         copy.wait_send()
     for p in range(PAIRS):
-        @pl.when(p != dp)
+        @pl.when(owner_of(p) != dp)
         def _():
             q_copy(p).wait_send()
             kv_copy(p).wait_send()
@@ -628,30 +648,36 @@
         def _():
             oy(step).wait_send()
 
-    @pl.when(dp < PAIRS)
+    @pl.when(owns_tokens)
     def _():
         for step in range(1, 4):
             @pl.when(other_x(step) < 3)
             def _():
                 tok(step, lax.min(other_x(step), 2)).wait_send()
-        for i in range(2):
-            @pl.when(oz_step(i) != 0)
-            def _():
-                oz(i).wait_send()
 
         @pl.when(x < 3)
         def _():
             for half in range(2):
                 for step in range(1, 8):
                     zs(step, half).wait_send()
+                    fin(step, half).wait_send()
+
+    @pl.when(dp < PAIRS)
+    def _():
+        for i in range(2):
+            @pl.when(oz_step(i) != 0)
+            def _():
+                oz(i).wait_send()
 
         @pl.when((z // 2 == x) & (x < 3))
         def _():
             out_fin().wait_send()
 
-        for half in range(2):
-            for step in range(1, 8):
-                fin(step, half).wait_send()
+        @pl.when(x == 3)
+        def _():
+            for half in range(2):
+                for step in range(1, 8):
+                    fin(step, half).wait_send()
 
 
 def finish(gin_ref, pieces_ref, gin_out, wg_out):

time: 65 us -> 65.2 us (level)
  no operation moved by 1% of the time
where the time goes in v7:
time: 65.2 us; the launch traced here: 64.3 us
  Pallas kernels  63.7 us (98%)
    pallas_call x1, Pallas kernels, on_device(): pl.pallas_call(kernel, out_shape=(jax.ShapeDtypeStruct((B, D), BF), jax.S...  61.9 us
    pallas_call x1, Pallas kernels, on_device(): pl.pallas_call(finish, out_shape=(jax.ShapeDtypeStruct((B, D), BF), jax.S...  1.8 us

profile of v7, /device:TPU:1, one launch (start us, length us, event | category | flops | bytes accessed | tf_op | source)
XLA Modules:
  0.0 64.3 jit_solution(1448783965622395629)
XLA Ops:
  0.6 61.9 %shard_map.131 = (bf16[128,768]{1,0:T(8,128)(2,1)}, bf16[6,96,128]{2,1,0:T(8,128)(2,1)}) custom-call(s32[1,128]{1,0:T(1,128)} %ids_ref.1, bf16[128,768]{1,0:T(8,128)(2,1)} %bitcast.2, bf16[256,768]{1,0:T(8,128)(2,1)} %table_hbm.1, bf16[768,768]{1,0:T(8,128)(2,1)} %wq_hbm.1, bf16[768,768]{1,0:T(8,128)(2,1)} %wk_hbm.1, bf16[768,768]{1,0:T(8,128)(2,1)} %wv_hbm.1, ...), custom_call_target="tpu_custom_call" | custom-call | tf_op jit(solution)/shard_map/pallas_call | solution.py:695
  62.5 1.8 %shard_map.132 = (bf16[128,768]{1,0:T(8,128)(2,1)}, f32[96,768]{1,0:T(8,128)}) custom-call(bf16[128,768]{1,0:T(8,128)(2,1)} %get-tuple-element.6.gin_ref, bf16[6,96,128]{2,1,0:T(8,128)(2,1)} %get-tuple-element.7.pieces_ref), custom_call_target="tpu_custom_call" | custom-call | tf_op jit(solution)/shard_map/pallas_call | solution.py:760

commit v8 on v6

--- a/solution.py
+++ b/solution.py
@@ -181,12 +181,12 @@
     project_table(wk, ktab)
     loads[3].wait()
     project_table(wv, vtab)
-    forward(1, 0)
     loads[4].wait()
     project_table(wq, qtab)
     loads[5].wait()
     loads[1].wait()
     gatt[pl.ds(0, B), :] = nt(cot_all[0], wo[...]).astype(BF)
+    forward(1, 0)
 
     far = 1 << 20
     dist = lax.broadcasted_iota(jnp.int32, (B, SPAN), 0) + WINDOW - lax.broadcasted_iota(jnp.int32, (B, SPAN), 1)
@@ -356,11 +356,12 @@
 
     lax.fori_loop(0, PAIRS // 2, pass_one_pairs, 0)
 
+    forward(3, 1)
     stats[1, 0] = statc[...].T[16:32]
     for d in range(REACH, 0, -1):
         stat_copy(1, d).start()
-    forward(3, 1)
-    out_terms(0, D, (0, 3))
+    out_terms(0, 2 * B, (0,))
+    out_terms(4 * B, 2 * B, (3,))
     out_core_sum((1, 2))
 
     ntab_t[...] = ntab[...].T

time: 65 us -> 65.4 us (level)
  no operation moved by 1% of the time
where the time goes in v8:
time: 65.4 us; the launch traced here: 64.6 us
  Pallas kernels  64 us (98%)
    pallas_call x1, Pallas kernels, on_device(): pl.pallas_call(kernel, out_shape=(jax.ShapeDtypeStruct((B, D), BF), jax.S...  62.2 us
    pallas_call x1, Pallas kernels, on_device(): pl.pallas_call(finish, out_shape=(jax.ShapeDtypeStruct((B, D), BF), jax.S...  1.8 us

profile of v8, /device:TPU:1, one launch (start us, length us, event | category | flops | bytes accessed | tf_op | source)
XLA Modules:
  0.0 64.6 jit_solution(6879563826448025659)
XLA Ops:
  0.6 62.2 %shard_map.131 = (bf16[128,768]{1,0:T(8,128)(2,1)}, bf16[6,96,128]{2,1,0:T(8,128)(2,1)}) custom-call(s32[1,128]{1,0:T(1,128)} %ids_ref.1, bf16[128,768]{1,0:T(8,128)(2,1)} %bitcast.2, bf16[256,768]{1,0:T(8,128)(2,1)} %table_hbm.1, bf16[768,768]{1,0:T(8,128)(2,1)} %wq_hbm.1, bf16[768,768]{1,0:T(8,128)(2,1)} %wk_hbm.1, bf16[768,768]{1,0:T(8,128)(2,1)} %wv_hbm.1, ...), custom_call_target="tpu_custom_call" | custom-call | tf_op jit(solution)/shard_map/pallas_call | solution.py:670
  62.8 1.8 %shard_map.132 = (bf16[128,768]{1,0:T(8,128)(2,1)}, f32[96,768]{1,0:T(8,128)}) custom-call(bf16[128,768]{1,0:T(8,128)(2,1)} %get-tuple-element.6.gin_ref, bf16[6,96,128]{2,1,0:T(8,128)(2,1)} %get-tuple-element.7.pieces_ref), custom_call_target="tpu_custom_call" | custom-call | tf_op jit(solution)/shard_map/pallas_call | solution.py:735

commit v9 on v6

--- a/solution.py
+++ b/solution.py
@@ -506,6 +506,14 @@
 
     lax.fori_loop(0, PAIRS // 2, pass_two_pairs, 0)
 
+    grad_normed = nt(gq[...], wq[...]) + nt(gk[...], wk[...]) + nt(gv[...], wv[...])
+    own = emb[...]
+    inv = lax.rsqrt(jnp.mean(own * own, axis=1, keepdims=True) + EPSILON)
+    scaled = own * inv
+    gin_ref[...] = (
+        inv * (grad_normed - scaled * jnp.mean(grad_normed * scaled, axis=1, keepdims=True))
+    ).astype(BF)
+
     for step in range(1, 4):
         ox(step).wait_recv()
     for row in range(3):
@@ -517,14 +525,6 @@
         @pl.when(other_y(step) < 3)
         def _():
             oy(step).start()
-
-    grad_normed = nt(gq[...], wq[...]) + nt(gk[...], wk[...]) + nt(gv[...], wv[...])
-    own = emb[...]
-    inv = lax.rsqrt(jnp.mean(own * own, axis=1, keepdims=True) + EPSILON)
-    scaled = own * inv
-    gin_ref[...] = (
-        inv * (grad_normed - scaled * jnp.mean(grad_normed * scaled, axis=1, keepdims=True))
-    ).astype(BF)
 
     @pl.when(dp < PAIRS)
     def _():

time: 65 us -> 65 us (level)
  no operation moved by 1% of the time
where the time goes in v9:
time: 65 us; the launch traced here: 64.6 us
  Pallas kernels  63.9 us (98%)
    pallas_call x1, Pallas kernels, on_device(): pl.pallas_call(kernel, out_shape=(jax.ShapeDtypeStruct((B, D), BF), jax.S...  62.1 us
    pallas_call x1, Pallas kernels, on_device(): pl.pallas_call(finish, out_shape=(jax.ShapeDtypeStruct((B, D), BF), jax.S...  1.8 us

profile of v9, /device:TPU:1, one launch (start us, length us, event | category | flops | bytes accessed | tf_op | source)
XLA Modules:
  0.0 64.6 jit_solution(11443264123003421252)
XLA Ops:
  0.6 62.1 %shard_map.131 = (bf16[128,768]{1,0:T(8,128)(2,1)}, bf16[6,96,128]{2,1,0:T(8,128)(2,1)}) custom-call(s32[1,128]{1,0:T(1,128)} %ids_ref.1, bf16[128,768]{1,0:T(8,128)(2,1)} %bitcast.2, bf16[256,768]{1,0:T(8,128)(2,1)} %table_hbm.1, bf16[768,768]{1,0:T(8,128)(2,1)} %wq_hbm.1, bf16[768,768]{1,0:T(8,128)(2,1)} %wk_hbm.1, bf16[768,768]{1,0:T(8,128)(2,1)} %wv_hbm.1, ...), custom_call_target="tpu_custom_call" | custom-call | tf_op jit(solution)/shard_map/pallas_call | solution.py:669
  62.8 1.8 %shard_map.132 = (bf16[128,768]{1,0:T(8,128)(2,1)}, f32[96,768]{1,0:T(8,128)}) custom-call(bf16[128,768]{1,0:T(8,128)(2,1)} %get-tuple-element.6.gin_ref, bf16[6,96,128]{2,1,0:T(8,128)(2,1)} %get-tuple-element.7.pieces_ref), custom_call_target="tpu_custom_call" | custom-call | tf_op jit(solution)/shard_map/pallas_call | solution.py:734
